TPU v7x, 32 devices: a whole 2x2x4 slice. The times are simulated.
32 devices in a mesh: gx: 8 (over z, x), gy: 4 (over y, core).
Axes of the slice: x: 2, y: 2, z: 4, core: 2. Of those that a mesh axis runs over, the one named last changes fastest.
Arguments:
- coarse_pop: float32 [9, 8192, 512], P(None, 'gx', 'gy'), may hold values from 0.001 to 1, as said below
- fine_pop: float32 [512, 9, 4096], P(('gx', 'gy')), may hold values from 0.001 to 1, as said below
- fine_block: int32 [512], P(('gx', 'gy')), may hold values from 0 to 4095, as said below
Outputs:
- coarse_out: float32 [9, 8192, 512], P(None, 'gx', 'gy')
- fine_out: float32 [512, 9, 4096], P(('gx', 'gy'))
Inputs may be any that keep to these rules, and one draw needn't show every extreme that they name: `coarse_pop`: populations of a state near equilibrium, positive. `fine_pop`: populations of a state near equilibrium, positive. `fine_block`: the slots of the device at (gx, gy) name distinct blocks whose rows lie in the gy-th band of 4 rows; no block is named twice; of one device's slots, at most 2 name blocks whose columns lie in the band of 32 columns of any one gx index, and this bound is reached for every device.
All inputs are finite; a program needn't handle non-finite values.
Results may differ from a plain program's by a relative error of at most 0.0003.
Values sent between devices are 32-bit elements; how exact they have to be, the bound alone decides.
No kernel may reach another device: no remote copies, remote signals or barrier semaphores. Data moves between devices by JAX's collectives and lax.ppermute only.
A program may use at most 192 MiB of HBM per device.

v0:
```python
import jax
import jax.numpy as jnp
from jax import lax
from jax.sharding import PartitionSpec as P

FINE_EDGE = 64
COARSE_EDGE = 32
CAP = 2


along_x = [0, 1, 0, -1, 0, 1, -1, -1, 1]
along_y = [0, 0, 1, 0, -1, 1, 1, -1, -1]
opposite = [0, 3, 4, 1, 2, 7, 8, 5, 6]
lattice_weights = [
    4.0 / 9,
    1.0 / 9,
    1.0 / 9,
    1.0 / 9,
    1.0 / 9,
    1.0 / 36,
    1.0 / 36,
    1.0 / 36,
    1.0 / 36,
]
moment_list = [
    [1.0, 1, 1, 1, 1, 1, 1, 1, 1],
    [-4, -1, -1, -1, -1, 2, 2, 2, 2],
    [4, -2, -2, -2, -2, 1, 1, 1, 1],
    [0, 1, 0, -1, 0, 1, -1, -1, 1],
    [0, -2, 0, 2, 0, 1, -1, -1, 1],
    [0, 0, 1, 0, -1, 1, 1, -1, -1],
    [0, 0, -2, 0, 2, 1, 1, -1, -1],
    [0, 1, -1, 1, -1, 0, 0, 0, 0],
    [0, 0, 0, 0, 0, 1, -1, 1, -1],
]
fine_relax = 0.8
coarse_relax = 0.65
explode_factor = 0.8 / 1.3
coalesce_factor = 1.3 / 0.8


def with_halo(block, sides, width):
    for axis, dim in sides:
        count = lax.axis_size(axis)
        forward = [(i, i + 1) for i in range(count - 1)]
        forward.append((count - 1, 0))
        backward = [(target, source) for source, target in forward]
        low = lax.ppermute(
            lax.slice_in_dim(block, block.shape[dim] - width, None, axis=dim), axis, forward
        )
        high = lax.ppermute(lax.slice_in_dim(block, 0, width, axis=dim), axis, backward)
        block = jnp.concatenate([low, block, high], axis=dim)
    return block


def mrt_table(relax_time):
    rates = [0.0, 1.4, 1.4, 0.0, 1.2, 0.0, 1.2, 1.0 / relax_time, 1.0 / relax_time]
    norms = [sum((float(value) * float(value) for value in moment_list[k])) for k in range(9)]
    table = []
    for first in range(9):
        line = []
        for second in range(9):
            total = 0.0
            for k in range(9):
                total = total + float(moment_list[k][first]) / norms[k] * rates[k] * float(
                    moment_list[k][second]
                )
            line.append(total)
        table.append(line)
    return table


def macroscopic(popul):
    step_x = jnp.asarray(along_x, jnp.float32)[:, None]
    step_y = jnp.asarray(along_y, jnp.float32)[:, None]
    density = jnp.sum(popul, axis=-2)
    speed_x = jnp.sum(popul * step_x, axis=-2) / density
    speed_y = jnp.sum(popul * step_y, axis=-2) / density
    return (density, speed_x, speed_y)


def equilibrium(density, speed_x, speed_y):
    step_x = jnp.asarray(along_x, jnp.float32)[:, None]
    step_y = jnp.asarray(along_y, jnp.float32)[:, None]
    weights = jnp.asarray(lattice_weights, jnp.float32)[:, None]
    projected = step_x * speed_x[..., None, :] + step_y * speed_y[..., None, :]
    squared = (speed_x * speed_x + speed_y * speed_y)[..., None, :]
    return (
        weights
        * density[..., None, :]
        * (1.0 + 3.0 * projected + 4.5 * projected * projected - 1.5 * squared)
    )


def collide(popul, relax_time):
    balance = equilibrium(*macroscopic(popul))
    matrix = jnp.asarray(mrt_table(relax_time), jnp.float32)
    return popul - jnp.einsum(
        "ij,...jn->...in", matrix, popul - balance, precision=lax.Precision.HIGHEST
    )


def rescale(popul, factor):
    balance = equilibrium(*macroscopic(popul))
    return balance + factor * (popul - balance)


def stream_coarse(collided, base_y, total_y):
    width_x = collided.shape[1] - 2
    width_y = collided.shape[2] - 2
    coord_y = jnp.arange(width_y, dtype=jnp.int32) + base_y - 1
    result = []
    for direction in range(9):
        shift_x = int(along_x[direction])
        shift_y = int(along_y[direction])
        source = collided[
            direction, 1 - shift_x : 1 - shift_x + width_x, 1 - shift_y : 1 - shift_y + width_y
        ]
        bounced = collided[opposite[direction], 1 : 1 + width_x, 1 : 1 + width_y]
        beyond = (coord_y - shift_y < 0) | (coord_y - shift_y >= total_y)
        result.append(jnp.where(beyond[None, :], bounced, source))
    return jnp.stack(result)


def cycle_of(square):
    return jnp.stack(
        [square[..., 0, :], square[..., -1, :], square[..., :, 0], square[..., :, -1]], axis=-2
    )


def widen(border):
    return jnp.concatenate(
        [border[..., :1], jnp.repeat(border[..., 1:-1], 2, axis=-1), border[..., -1:]], axis=-1
    )


def fine_substep(interior, cycle_pre, low_wall, high_wall):
    slot_count = interior.shape[0]
    edge_len = interior.shape[-1]
    cycle_len = cycle_pre.shape[-1]
    ghost_pre = rescale(cycle_pre.reshape(slot_count, 9, 4 * cycle_len), explode_factor)
    ghosts = collide(ghost_pre, fine_relax).reshape(slot_count, 9, 4, cycle_len)
    inner = collide(interior.reshape(slot_count, 9, edge_len * edge_len), fine_relax).reshape(
        slot_count, 9, edge_len, edge_len
    )
    upper_row = widen(ghosts[:, :, 0])
    lower_row = widen(ghosts[:, :, 1])
    left_col = widen(ghosts[:, :, 2])
    right_col = widen(ghosts[:, :, 3])
    middle = jnp.concatenate(
        [left_col[:, :, 1:-1, None], inner, right_col[:, :, 1:-1, None]], axis=3
    )
    padded = jnp.concatenate([upper_row[:, :, None, :], middle, lower_row[:, :, None, :]], axis=2)
    coord_y = jnp.arange(edge_len, dtype=jnp.int32)
    result = []
    for direction in range(9):
        shift_x = int(along_x[direction])
        shift_y = int(along_y[direction])
        source = padded[
            :, direction, 1 - shift_x : 1 - shift_x + edge_len, 1 - shift_y : 1 - shift_y + edge_len
        ]
        bounced = inner[:, opposite[direction]]
        beyond = (
            low_wall[:, None] & (coord_y - shift_y < 0)[None, :]
            | high_wall[:, None] & (coord_y - shift_y >= edge_len)[None, :]
        )
        result.append(jnp.where(beyond[:, None, :], bounced, source))
    return jnp.stack(result, axis=1)


def coalesce(interior):
    slot_count = interior.shape[0]
    half = interior.shape[-1] // 2
    grouped = interior.reshape(slot_count, 9, half, 2, half, 2)
    average = jnp.sum(grouped, axis=(3, 5)) * 0.25
    return rescale(average.reshape(slot_count, 9, half * half), coalesce_factor)


def fine_advance(interior, cycles, low_wall, high_wall):
    old_cycle = cycles[:, 0]
    new_cycle = cycles[:, 1]
    first = fine_substep(interior, old_cycle, low_wall, high_wall)
    second = fine_substep(first, 0.5 * (old_cycle + new_cycle), low_wall, high_wall)
    return (second, coalesce(second))


def cut_square(field, start_x, start_y):
    cycle_len = COARSE_EDGE + 2
    zero = jnp.zeros((), jnp.int32)
    return lax.dynamic_slice(field, (zero, start_x, start_y), (9, cycle_len, cycle_len))


def local(coarse_pop, fine_pop, fine_block):
    width_x = coarse_pop.shape[1]
    width_y = coarse_pop.shape[2]
    blocks_x = width_x // COARSE_EDGE
    blocks_y = width_y // COARSE_EDGE
    count_x = lax.axis_size("gx")
    count_y = lax.axis_size("gy")
    index_x = lax.axis_index("gx")
    index_y = lax.axis_index("gy")
    column_blocks = blocks_y * count_y
    cycle_len = COARSE_EDGE + 2
    padded_two = with_halo(coarse_pop, (("gx", 1), ("gy", 2)), 2)
    collided = collide(padded_two.reshape(9, -1), coarse_relax).reshape(padded_two.shape)
    new_one = stream_coarse(collided, index_y * width_y, width_y * count_y)
    old_one = padded_two[:, 1:-1, 1:-1]
    coarse_next = new_one[:, 1:-1, 1:-1]
    slot_count = fine_block.shape[0]
    all_map = lax.all_gather(fine_block, "gx", axis=0, tiled=True).reshape(count_x, slot_count)
    block_col = all_map // column_blocks
    block_row = all_map % column_blocks
    owner = block_col // blocks_x
    local_id = block_col % blocks_x * blocks_y + block_row % blocks_y
    slot_ids = jnp.arange(slot_count, dtype=jnp.int32)
    earlier = slot_ids[None, :] < slot_ids[:, None]
    same_owner = owner[:, :, None] == owner[:, None, :]
    ranking = jnp.sum((same_owner & earlier[None]).astype(jnp.int32), axis=2)
    from_here = owner == index_x
    placed = (ranking[:, :, None] == jnp.arange(CAP, dtype=jnp.int32)[None, None, :]) & from_here[
        :, :, None
    ]
    send_local = jnp.sum(jnp.where(placed, local_id[:, :, None], 0), axis=1)
    send_live = jnp.any(placed, axis=1)
    my_owner = owner[index_x]
    my_rank = ranking[index_x]
    my_row = fine_block % column_blocks
    flat_local = send_local.reshape(-1)
    start_x = flat_local // blocks_y * COARSE_EDGE
    start_y = flat_local % blocks_y * COARSE_EDGE
    old_cut = jax.vmap(lambda first_x, first_y: cut_square(old_one, first_x, first_y))(
        start_x, start_y
    )
    new_cut = jax.vmap(lambda first_x, first_y: cut_square(new_one, first_x, first_y))(
        start_x, start_y
    )
    stacked = jnp.stack([old_cut, new_cut], axis=1)
    outgoing = stacked.reshape(count_x, CAP, -1)
    incoming = lax.all_to_all(outgoing, "gx", split_axis=0, concat_axis=0, tiled=True)
    picked = incoming[my_owner, my_rank]
    cycles = cycle_of(picked.reshape(slot_count, 2, 9, cycle_len, cycle_len))
    interior = fine_pop.reshape(slot_count, 9, FINE_EDGE, FINE_EDGE)
    fine_next, merged = fine_advance(interior, cycles, my_row == 0, my_row == column_blocks - 1)
    block_size = 9 * COARSE_EDGE * COARSE_EDGE
    back_buffer = (
        jnp.zeros((count_x, CAP, block_size), jnp.float32)
        .at[my_owner, my_rank]
        .set(merged.reshape(slot_count, block_size))
    )
    returned = lax.all_to_all(back_buffer, "gx", split_axis=0, concat_axis=0, tiled=True)
    blocks = (
        coarse_next.reshape(9, blocks_x, COARSE_EDGE, blocks_y, COARSE_EDGE)
        .transpose(1, 3, 0, 2, 4)
        .reshape(blocks_x * blocks_y, block_size)
    )
    target = jnp.where(send_live, send_local, blocks_x * blocks_y).reshape(-1)
    blocks = blocks.at[target].set(returned.reshape(count_x * CAP, block_size), mode="drop")
    coarse_out = (
        blocks.reshape(blocks_x, blocks_y, 9, COARSE_EDGE, COARSE_EDGE)
        .transpose(2, 0, 3, 1, 4)
        .reshape(9, width_x, width_y)
    )
    return (coarse_out, fine_next.reshape(slot_count, 9, FINE_EDGE * FINE_EDGE))


def solution(mesh):
    return jax.shard_map(
        local,
        mesh=mesh,
        in_specs=(P(None, "gx", "gy"), P(("gx", "gy"), None, None), P(("gx", "gy"))),
        out_specs=(P(None, "gx", "gy"), P(("gx", "gy"), None, None)),
        check_vma=False,
    )
```

profile of v0, /device:TPU:0, one launch (start us, length us, event | category | flops | bytes accessed | tf_op | source)
XLA Modules:
  0.0 638.0 jit_solution(15465917598248891470)
XLA Ops:
  1.6 3.0 collective-permute-start
  4.6 3.1 collective-permute-start.1
  10.5 9.9 %all-reduce = s32[128]{0:T(128)S(1)} all-reduce(s32[128]{0:T(128)S(1)} %dynamic-update-slice.4), channel_id=1, replica_groups=mesh['gx'=8,'gy'=4] {'gx'}, use_global_device_ids=true, to_apply=%add | all-reduce | flops 128 | bytes 1024
  25.4 7.6 %fusion.23 = f32[16,4096,9]{1,2,0:T(8,128)} fusion(f32[9,9,1]{1,0,2:T(8,128)S(1)} %copy-done.32, f32[16,9,4096]{2,0,1:T(8,128)S(1)} %fusion.28), kind=kOutput, calls=%fused_computation.39 | convolution fusion | flops 63700992 | bytes 4718916 | tf_op jit(solution)/shard_map/ij,...jn->...in/dot_general | solution.py:98
  33.1 6.0 copy.382
  39.7 6.8 %concatenate.69 = f32[9,1028,128]{1,2,0:T(8,128)} concatenate(f32[9,2,128]{1,2,0:T(8,128)S(1)} %copy.381, f32[9,1024,128]{1,2,0:T(8,128)} %copy.382, f32[9,2,128]{1,2,0:T(8,128)S(1)} %copy.383), dimensions={1} | concatenate | bytes 9474048 | tf_op jit(solution)/shard_map/concatenate | solution.py:52
  51.7 6.6 %multiply_reduce_fusion.1 = (f32[1028,132]{0,1:T(8,128)S(1)}, f32[1028,132]{0,1:T(8,128)S(1)}, f32[1028,132]{0,1:T(8,128)S(1)}, f32[9,1028,132]{1,2,0:T(8,128)}) fusion(f32[9]{0:T(128)S(1)} %copy-done.28, f32[9,1028,2]{1,2,0:T(2,128)S(1)} %collective-permute-done.3, f32[9,1028,128]{1,2,0:T(8,128)} %concatenate.69, ...), kind=kLoop, calls=%fused_computation.24 | loop fusion | flops 8141760 | bytes 11398536 | tf_op jit(solution)/shard_map/reduce_sum | solution.py:77
  58.3 8.7 %copy.384 = f32[9,1028,132]{2,1,0:T(8,128)} copy(f32[9,1028,132]{1,2,0:T(8,128)} %get-tuple-element.144) | data formatting | bytes 9770112 | tf_op jit(solution)/shard_map/concatenate | solution.py:52
  67.0 7.3 %slice.423 = f32[9,1026,130]{1,2,0:T(8,128)} slice(f32[9,1028,132]{1,2,0:T(8,128)} %get-tuple-element.144), slice={[0:9], [1:1027], [1:131]} | slice | bytes 9603360 | tf_op jit(solution)/shard_map/slice | solution.py:207
  77.6 15.7 %reshape.1244 = f32[9,135696]{1,0:T(8,128)} reshape(f32[9,1028,132]{2,1,0:T(8,128)} %copy.384) | data formatting | bytes 9770112 | tf_op jit(solution)/shard_map/reshape | solution.py:205
  94.0 17.2 %convolution_subtract_fusion = f32[9,135696]{1,0:T(8,128)} fusion(f32[9,135696]{1,0:T(8,128)} %reshape.1244, f32[9,9]{1,0:T(8,128)S(1)} %copy-done.43, f32[135696]{0:T(1024)S(1)} %get-tuple-element.127, f32[135696]{0:T(1024)S(1)} %get-tuple-element.129, f32[9]{0:T(128)S(1)} %copy-done.30, f32[135696]{0:T(1024)S(1)} %get-tuple-element.128, ...), kind=kOutput, calls=%fused_computation.8 | convolution fusion | flops 147772944 | bytes 11941680 | tf_op jit(solution)/shard_map/ij,...jn->...in/dot_general | solution.py:98
  111.2 15.8 %reshape.1245 = f32[9,1028,132]{2,1,0:T(8,128)} reshape(f32[9,135696]{1,0:T(8,128)} %convolution_subtract_fusion) | data formatting | bytes 9770112 | tf_op jit(solution)/shard_map/reshape | solution.py:205
  138.2 3.5 copy-done.10
  141.7 49.1 %while.3 = (s32[]{:T(128)}, f32[9,1026,130]{2,1,0:T(8,128)}, s32[16,3]{0,1:T(4,128)S(1)}, f32[16,9,34,34]{3,2,1,0:T(8,128)S(1)}, s32[]{:T(128)}) while((s32[]{:T(128)}, f32[9,1026,130]{2,1,0:T(8,128)}, s32[16,3]{0,1:T(4,128)S(1)}, f32[16,9,34,34]{3,2,1,0:T(8,128)S(1)}, s32[]{:T(128)}) %tuple.138), condition=%wide.while_cond.1, body=%wide.while_body.1.sunk | while | flops 2 | bytes 226053 | solution.py:190
  192.6 62.3 %while.2 = (s32[]{:T(128)}, f32[9,1026,130]{1,2,0:T(8,128)}, s32[16,3]{0,1:T(4,128)S(1)}, f32[16,9,34,34]{3,2,1,0:T(8,128)}, s32[]{:T(128)}) while((s32[]{:T(128)}, f32[9,1026,130]{1,2,0:T(8,128)}, s32[16,3]{0,1:T(4,128)S(1)}, f32[16,9,34,34]{3,2,1,0:T(8,128)}, s32[]{:T(128)}) %tuple.139), condition=%wide.while_cond, body=%wide.while_body.sunk | while | flops 2 | bytes 393025 | solution.py:190
  193.2 2.4 constant_dynamic-slice_fusion.7
  197.1 2.4 constant_dynamic-slice_fusion.7
  204.9 2.4 constant_dynamic-slice_fusion.7
  212.7 2.4 constant_dynamic-slice_fusion.7
  220.5 2.4 constant_dynamic-slice_fusion.7
  228.2 2.4 constant_dynamic-slice_fusion.7
  232.1 2.4 constant_dynamic-slice_fusion.7
  257.1 3.0 copy.394
  260.1 6.4 %reshape.1250 = f32[8,2,20808]{2,1,0:T(2,128)} reshape(f32[16,2,9,34,34]{4,3,2,1,0:T(8,128)} %copy.394) | data formatting | bytes 2663424 | tf_op jit(solution)/shard_map/reshape | solution.py:238
  266.5 3.7 all-to-all-start
  270.3 5.8 bitcast_subtract_fusion.1
  276.1 5.3 reshape.1249
  286.2 7.2 %slice.420 = f32[9,1024,128]{2,1,0:T(8,128)} slice(f32[9,1026,130]{2,1,0:T(8,128)} %get-tuple-element.280), slice={[0:9], [1:1025], [1:129]} | slice | bytes 9437184 | tf_op jit(solution)/shard_map/slice | solution.py:208
  293.3 14.2 %reshape.1246 = f32[9,32,32,4,32]{4,3,2,1,0:T(4,128)} reshape(f32[9,1024,128]{2,1,0:T(8,128)} %slice.420) | data formatting | bytes 9437184 | tf_op jit(solution)/shard_map/reshape | solution.py:252
  307.6 14.1 %copy.466 = f32[9,32,32,4,32]{4,2,0,3,1:T(8,128)} copy(f32[9,32,32,4,32]{4,3,2,1,0:T(4,128)} %reshape.1246) | data formatting | bytes 9437184 | tf_op jit(solution)/shard_map/reshape | solution.py:252
  321.6 14.0 %reshape.1247 = f32[128,9216]{1,0:T(8,128)} reshape(f32[32,4,9,32,32]{4,3,2,1,0:T(8,128)} %bitcast.202) | data formatting | bytes 9437184 | tf_op jit(solution)/shard_map/reshape | solution.py:254
  335.6 2.5 gather_fusion
  338.1 5.3 reshape.1251
  343.4 10.3 %fusion.181 = (f32[16,2,9,34,1]{4,3,2,1,0:T(8,128)}, f32[16,2,9,34,1]{4,3,2,1,0:T(8,128)}) fusion(f32[16,2,9,34,34]{4,3,2,1,0:T(8,128)} %reshape.1251), kind=kLoop, calls=%fused_computation.346 | loop fusion | bytes 156672 | tf_op jit(solution)/shard_map/slice | solution.py:127
  355.6 4.1 copy.395
  359.8 4.1 copy.396
  374.9 5.4 copy.406
  380.7 5.6 copy.407
  386.5 9.2 %add_add_fusion = (f32[16,1,64,64]{3,2,0,1:T(8,128)S(1)}, f32[16,1,64,64]{3,2,0,1:T(8,128)}, f32[16,1,64,64]{3,2,0,1:T(8,128)}, f32[16,1,64,64]{3,2,0,1:T(8,128)...) fusion(f32[16,9,64,64]{3,2,0,1:T(8,128)} %reshape.1249, ...), kind=kLoop, calls=%fused_computation.118 | loop fusion | flops 2359296 | bytes 21312768 | tf_op jit(solution)/shard_map/reduce_sum | solution.py:76
  418.8 6.9 %fusion.21 = f32[16,4096,9]{1,2,0:T(8,128)S(1)} fusion(f32[9,9,1]{1,0,2:T(8,128)S(1)} %copy-done.33, f32[16,9,4096]{2,0,1:T(8,128)S(1)} %fusion.32), kind=kOutput, calls=%fused_computation.37 | convolution fusion | flops 63700992 | bytes 4718916 | tf_op jit(solution)/shard_map/ij,...jn->...in/dot_general | solution.py:98
  425.7 2.9 bitcast_subtract_fusion
  428.6 5.3 reshape.1255
  434.3 5.8 copy.425
  440.4 5.4 copy.426
  446.2 3.3 fusion.48
  449.6 4.1 fusion.47
  460.5 5.6 fusion.46
  468.1 3.0 copy.416
  473.0 3.0 copy.428
  477.9 3.0 copy.436
  482.9 3.0 copy.437
  487.8 3.0 copy.438
  492.5 3.2 constant_dynamic-update-slice_fusion.17
  499.6 3.3 constant_dynamic-update-slice_fusion.16
  515.9 19.8 %reduce_sum.396 = f32[16,9,32,32]{0,3,2,1:T(8,128)} reduce(f32[16,9,32,2,32,2]{0,5,4,3,2,1:T(2,128)} %constant_dynamic-update-slice_fusion.9, f32[]{:T(128)} %constant.139.clone.1), dimensions={3,5}, to_apply=%region_23.24 | reduce | flops 442368 | bytes 2949124 | tf_op jit(solution)/shard_map/reduce_sum | solution.py:175
  535.7 6.0 multiply_reduce_fusion.3
  545.8 3.7 copy.444
  552.3 6.2 scatter_fusion
  558.5 6.1 all-to-all-start.1
  571.7 10.2 %all-to-all-done.1 = f32[8,2,9216]{2,1,0:T(2,128)S(1)} async-done(((f32[8,2,9216]{2,1,0:T(2,128)}), f32[8,2,9216]{2,1,0:T(2,128)S(1)}, u32[]{:S(2)}, u32[]{:S(2)}) %all-to-all-start.1) | async-done | bytes 589856 | tf_op jit(solution)/shard_map/all_to_all | solution.py:250
  582.3 5.4 scatter_fusion.1
  587.7 11.7 %reshape.1260 = f32[32,4,9,32,32]{4,3,2,1,0:T(8,128)} reshape(f32[128,9216]{1,0:T(8,128)} %scatter_fusion.1) | data formatting | bytes 9437184 | tf_op jit(solution)/shard_map/reshape | solution.py:259
  599.4 23.4 %copy.452 = f32[9,32,32,4,32]{4,3,2,1,0:T(4,128)} copy(f32[9,32,32,4,32]{4,2,0,3,1:T(8,128)} %bitcast.203) | data formatting | bytes 9437184
  622.8 14.9 %reshape.1340 = f32[9,1024,128]{2,1,0:T(8,128)} reshape(f32[9,32,32,4,32]{4,3,2,1,0:T(4,128)} %copy.452) | data formatting | bytes 9437184
  (416 shorter events, 218.2 us)
Async XLA Ops:
  0.6 23.8 %copy-start.28 = (f32[9]{0:T(128)S(1)}, f32[9]{0:T(128)}, u32[]{:S(2)}) copy-start(f32[9]{0:T(128)} %constant.170.clone) | copy-start | bytes 112
  0.6 23.8 %copy-start.30 = (f32[9]{0:T(128)S(1)}, f32[9]{0:T(128)}, u32[]{:S(2)}) copy-start(f32[9]{0:T(128)} %constant.171.clone) | copy-start | bytes 112
  0.7 23.8 %copy-start.36 = (f32[9]{0:T(128)S(1)}, f32[9]{0:T(128)}, u32[]{:S(2)}) copy-start(f32[9]{0:T(128)} %constant.172.clone) | copy-start | bytes 112
  0.7 23.8 %copy-start.2 = (f32[16,9,4096]{2,0,1:T(8,128)S(1)}, f32[16,9,4096]{2,0,1:T(8,128)}, u32[]{:S(2)}) copy-start(f32[16,9,4096]{2,0,1:T(8,128)} %param.49) | copy-start | bytes 7077892
  1.6 37.5 %collective-permute-start = (f32[9,2,128]{2,1,0:T(2,128)S(1)}, f32[9,2,128]{2,1,0:T(2,128)S(1)}, u32[]{:S(2)}, u32[]{:S(2)}) collective-permute-start(f32[9,2,128]{2,1,0:T(2,128)S(1)} %get-tuple-element.152), channel_id=1, source_target_pairs={{0,4},{4,8},{8,12},{12,16},{16,20},{20,24},{24,28},{28,0},{1,5},{5... | collective-permute-start | bytes 27656 | tf_op jit(solution)/shard_map/ppermute | solution.py:48
  4.6 34.8 %collective-permute-start.1 = (f32[9,2,128]{2,1,0:T(2,128)S(1)}, f32[9,2,128]{2,1,0:T(2,128)S(1)}, u32[]{:S(2)}, u32[]{:S(2)}) collective-permute-start(f32[9,2,128]{2,1,0:T(2,128)S(1)} %get-tuple-element.151), channel_id=1, source_target_pairs={{4,0},{8,4},{12,8},{16,12},{20,16},{24,20},{28,24},{0,28},{5,1},{9... | collective-permute-start | bytes 27656 | tf_op jit(solution)/shard_map/ppermute | solution.py:51
  24.4 1.0 copy-start.32
  47.7 3.9 collective-permute-start.2
  47.7 4.0 collective-permute-start.3
  93.3 0.7 copy-start.43
  128.5 6.9 %copy-start = (f32[9,1028,132]{2,1,0:T(8,128)S(1)}, f32[9,1028,132]{2,1,0:T(8,128)}, u32[]{:S(2)}) copy-start(f32[9,1028,132]{2,1,0:T(8,128)} %reshape.1245) | copy-start | bytes 14655172
  138.0 3.7 copy-start.10
  266.5 69.0 %all-to-all-start = ((f32[8,2,20808]{2,1,0:T(2,128)}), f32[8,2,20808]{2,1,0:T(2,128)S(1)}, u32[]{:S(2)}, u32[]{:S(2)}) async-start(f32[8,2,20808]{2,1,0:T(2,128)} %reshape.1250), calls=%async_computation | async-start | bytes 2670592 | tf_op jit(solution)/shard_map/all_to_all | solution.py:239
  276.1 9.2 %copy-start.42 = (s32[16]{0:T(128)S(1)}, s32[16]{0:T(128)}, u32[]{:S(2)}) copy-start(s32[16]{0:T(128)} %param.50) | copy-start | bytes 196
  285.4 101.0 %copy-start.24 = (pred[16,64]{1,0:T(8,128)(4,1)}, pred[16,64]{1,0:T(8,128)(4,1)S(1)}, u32[]{:S(2)}) copy-start(pred[16,64]{1,0:T(8,128)(4,1)S(1)} %get-tuple-element.179) | copy-start | bytes 3076
  285.4 101.0 %copy-start.26 = (pred[16,64]{1,0:T(8,128)(4,1)}, pred[16,64]{1,0:T(8,128)(4,1)S(1)}, u32[]{:S(2)}) copy-start(pred[16,64]{1,0:T(8,128)(4,1)S(1)} %get-tuple-element.180) | copy-start | bytes 3076
  285.4 101.0 %copy-start.34 = (pred[16,64]{1,0:T(8,128)(4,1)}, pred[16,64]{1,0:T(8,128)(4,1)S(1)}, u32[]{:S(2)}) copy-start(pred[16,64]{1,0:T(8,128)(4,1)S(1)} %get-tuple-element.181) | copy-start | bytes 3076
  359.8 4.9 copy-start.38
  359.8 4.9 copy-start.39
  396.6 12.2 %copy-start.1 = (f32[16,9,4096]{2,0,1:T(8,128)S(1)}, f32[16,9,4096]{2,0,1:T(8,128)}, u32[]{:S(2)}) copy-start(f32[16,9,4096]{2,0,1:T(8,128)} %constant_dynamic-update-slice_fusion.8) | copy-start | bytes 7077892
  408.8 5.9 copy-start.29
  408.8 5.9 copy-start.31
  417.1 1.7 copy-start.33
  440.0 5.7 copy-start.16
  440.3 5.8 copy-start.25
  440.3 5.8 copy-start.27
  446.0 3.6 slice-start
  446.1 3.3 copy-start.18
  446.1 3.3 copy-start.19
  446.1 3.4 slice-start.1
  446.1 3.4 copy-start.35
  453.6 0.8 copy-start.9
  454.6 4.6 copy-start.15
  454.6 4.9 copy-start.17
  499.6 3.3 copy-start.3
  504.4 2.3 copy-start.4
  505.9 2.4 copy-start.5
  508.3 2.3 copy-start.6
  509.7 2.3 copy-start.8
  512.1 2.3 copy-start.7
  515.9 19.8 %copy-start.40 = (f32[9]{0:T(128)S(1)}, f32[9]{0:T(128)}, u32[]{:S(2)}) copy-start(f32[9]{0:T(128)} %constant.209) | copy-start | bytes 112
  515.9 19.8 %copy-start.41 = (f32[9]{0:T(128)S(1)}, f32[9]{0:T(128)}, u32[]{:S(2)}) copy-start(f32[9]{0:T(128)} %constant.210) | copy-start | bytes 112
  545.8 3.7 copy-start.21
  545.8 3.7 copy-start.22
  545.8 3.7 copy-start.23
  549.6 2.7 copy-start.20
  552.3 14.0 %copy-start.11 = (f32[16,1,4096]{2,0,1:T(8,128)S(1)}, f32[16,1,4096]{2,0,1:T(8,128)}, u32[]{:S(2)}) copy-start(f32[16,1,4096]{2,0,1:T(8,128)} %stack.131) | copy-start | bytes 786436
  552.3 15.4 %copy-start.12 = (f32[16,1,4096]{2,0,1:T(8,128)S(1)}, f32[16,1,4096]{2,0,1:T(8,128)}, u32[]{:S(2)}) copy-start(f32[16,1,4096]{2,0,1:T(8,128)} %stack.133) | copy-start | bytes 786436
  558.5 9.9 %copy-start.13 = (f32[16,1,4096]{2,0,1:T(8,128)S(1)}, f32[16,1,4096]{2,0,1:T(8,128)}, u32[]{:S(2)}) copy-start(f32[16,1,4096]{2,0,1:T(8,128)} %stack.134) | copy-start | bytes 786436
  558.5 10.6 %copy-start.14 = (f32[16,1,4096]{2,0,1:T(8,128)S(1)}, f32[16,1,4096]{2,0,1:T(8,128)}, u32[]{:S(2)}) copy-start(f32[16,1,4096]{2,0,1:T(8,128)} %stack.135) | copy-start | bytes 786436
  558.5 23.3 %all-to-all-start.1 = ((f32[8,2,9216]{2,1,0:T(2,128)}), f32[8,2,9216]{2,1,0:T(2,128)S(1)}, u32[]{:S(2)}, u32[]{:S(2)}) async-start(f32[8,2,9216]{2,1,0:T(2,128)} %scatter_fusion), calls=%async_computation.1 | async-start | bytes 1179648 | tf_op jit(solution)/shard_map/all_to_all | solution.py:250
  567.0 15.3 %copy-start.37 = (s32[16]{0:T(128)S(1)}, s32[16]{0:T(128)}, u32[]{:S(2)}) copy-start(s32[16]{0:T(128)} %get-tuple-element.184) | copy-start | bytes 196
where the time goes:
time: 649 us; the launch traced here: 638 us
  local copies, waits for them, and re-layouts  472 us (73%)
  other arithmetic  89.7 us (14%)
  matrix products  33.3 us (5%)
  starting transfers between devices  17.9 us (3%)
  waiting for transfers between devices  12.2 us (2%)
  blocking collectives  9.94 us (2%)
    gather x128, local copies, waits for them, and re-layouts  111 us
    unnamed x129, local copies, waits for them, and re-layouts  90.3 us
    dot_general x5, matrix products, collide(): jnp.einsum('ij,...jn->...in', matrix, popul - balance, precision=lax.Prec...  33.3 us
    reshape x2, local copies, waits for them, and re-layouts, local(): coarse_next.reshape(9, blocks_x, COARSE_EDGE, blocks_y, COARSE_EDGE)  28.3 us
    another operation x21, local copies, waits for them, and re-layouts, fine_substep(): return jnp.stack(result, axis=1)  26.6 us
    reduce_sum x1, other arithmetic, coalesce(): average = jnp.sum(grouped, axis=(3, 5)) * 0.25  19.8 us
    select_n x8, local copies, waits for them, and re-layouts, fine_substep(): result.append(jnp.where(beyond[:, None, :], bounced, source))  19.6 us
    reduce_sum x6, other arithmetic, macroscopic(): speed_x = jnp.sum(popul * step_x, axis=-2) / density  17.2 us
  transfers between devices with their start and end apart: 6, of which 3 were waited for; matrix products, arithmetic and copies ran while one was open for 15% of the time, Pallas kernels for 0%

commit v1 on v0

v1 whole, which is shorter than its diff:
```python
import functools

import jax
import jax.numpy as jnp
from jax import lax
from jax.experimental import pallas as pl
from jax.experimental.pallas import tpu as pltpu
from jax.sharding import PartitionSpec as P

FINE_EDGE = 64
COARSE_EDGE = 32
CAP = 2
LANES = 128
WINDOW = 42

along_x = [0, 1, 0, -1, 0, 1, -1, -1, 1]
along_y = [0, 0, 1, 0, -1, 1, 1, -1, -1]
opposite = [0, 3, 4, 1, 2, 7, 8, 5, 6]
UP = (1, 5, 8)
DOWN = (3, 6, 7)
LEFT = (2, 5, 6)
RIGHT = (4, 8, 7)
ORDER = (0, 1, -1)

F32 = jnp.float32


def rates_of(relax_time, factor=1.0):
    return tuple((1.0 - factor) + factor * rate for rate in (1.4, 1.4, 1.2, 1.0 / relax_time))


COARSE = rates_of(0.65)
FINE = rates_of(0.8)
GHOST = rates_of(0.8, 0.8 / 1.3)
COALESCE = (1.0 - 1.3 / 0.8,) * 4


def relax(p, rates, which=tuple(range(9))):
    s_e, s_p, s_q, s_n = rates
    p0, p1, p2, p3, p4, p5, p6, p7, p8 = p
    s1, d1 = p1 + p3, p1 - p3
    s2, d2 = p2 + p4, p2 - p4
    s5, d5 = p5 + p7, p5 - p7
    s6, d6 = p6 + p8, p6 - p8
    axial, diagonal = s1 + s2, s5 + s6
    rho = p0 + axial + diagonal
    dq, sq = d5 - d6, d5 + d6
    jx, jy = d1 + dq, d2 + sq
    inv = 1.0 / rho
    xx, yy = jx * jx, jy * jy
    square = 3.0 * ((xx + yy) * inv)
    e = (axial - 2.0 * p0) + 4.0 * diagonal - square
    eps = 3.0 * (p0 - axial) + square
    a = (s_e / 36.0) * e
    b = (s_p / 36.0) * eps
    c = (s_q / 12.0) * (2.0 * dq - d1)
    d = (s_q / 12.0) * (2.0 * sq - d2)
    f = (s_n / 4.0) * ((s1 - s2) - (xx - yy) * inv)
    g = (s_n / 4.0) * ((s5 - s6) - (jx * jy) * inv)
    out = {}
    t = a + 2.0 * b
    w = 2.0 * a + b
    if 0 in which:
        out[0] = p0 + 4.0 * (a - b)
    if 1 in which:
        out[1] = p1 + ((t - f) + 2.0 * c)
    if 3 in which:
        out[3] = p3 + ((t - f) - 2.0 * c)
    if 2 in which:
        out[2] = p2 + ((t + f) + 2.0 * d)
    if 4 in which:
        out[4] = p4 + ((t + f) - 2.0 * d)
    if 5 in which:
        out[5] = p5 - ((w + g) + (c + d))
    if 7 in which:
        out[7] = p7 - ((w + g) - (c + d))
    if 6 in which:
        out[6] = p6 - ((w - g) - (c - d))
    if 8 in which:
        out[8] = p8 - ((w - g) + (c - d))
    return out


def lane_of(shape):
    return lax.broadcasted_iota(jnp.int32, shape, 1)


def row_of(shape):
    return lax.broadcasted_iota(jnp.int32, shape, 0)


def take_lanes(value, index):
    return jnp.take_along_axis(value, index, axis=1, mode="promise_in_bounds")


def table_kernel(columns, blocks_x, blocks_y, count_x, block_ref, id_ref, slot_ref, seen_ref):
    places = count_x * CAP
    for place in range(places):
        id_ref[place] = -1
        slot_ref[place] = -1
        slot_ref[places + place] = 0
    for owner in range(count_x):
        seen_ref[owner] = 0
    for slot in range(block_ref.shape[0]):
        block = block_ref[slot]
        column = lax.div(block, columns)
        row = block - column * columns
        owner = lax.div(column, blocks_x)
        rank = seen_ref[owner]
        seen_ref[owner] = rank + 1
        place = owner * CAP + rank
        id_ref[place] = (column - owner * blocks_x) * blocks_y + lax.rem(row, blocks_y)
        slot_ref[place] = slot
        slot_ref[places + place] = jnp.where(row == 0, 1, 0) + jnp.where(row == columns - 1, 2, 0)


def pack_kernel(coarse, low, high, sets, to_high, to_low, buf, ext, z, sems):
    width = coarse.shape[1]
    wide = width + LANES
    copies = [pltpu.make_async_copy(coarse.at[d], buf.at[d], sems.at[d]) for d in range(9)]
    for copy in copies:
        copy.start()
    ext[...] = jnp.full(ext.shape, 0.1, F32)
    ext[0, :, 0:2, :] = high[...]
    ext[1, :, 6:8, :] = low[...]
    z[:, width:, :] = jnp.full((2, LANES, LANES), 0.1, F32)
    rows = 64

    def columns_of(shape):
        lane = lane_of(shape)
        key = lax.rem(lane, 24)
        col = 32 * (key & 3) + (key >> 3) + jnp.where((key & 4) == 0, -2, 31)
        return lane, col & (LANES - 1)

    def place(group, part, start, count, value):
        lane, col = columns_of((count, LANES))
        got = take_lanes(value, col)
        if part:
            inside = (lane >= 24 * part) & (lane < 24 * part + 24)
            got = jnp.where(inside, got, z[group, pl.ds(start, count), :])
        z[group, pl.ds(start, count), :] = got

    for d in range(9):
        group, part = divmod(d, 5)
        place(group, part, width, 8, ext[0, d])
        place(group, part, wide - 8, 8, ext[1, d])
        copies[d].wait()

        def chunk(k, carry, group=group, part=part, d=d):
            start = pl.multiple_of(k * rows, rows)
            place(group, part, start, rows, buf[d, pl.ds(start, rows), :])
            return carry

        lax.fori_loop(0, width // rows, chunk, 0)
    to_high[...] = jnp.full(to_high.shape, 0.1, F32)
    to_low[...] = jnp.full(to_low.shape, 0.1, F32)
    for group in range(2):
        for t in range(wide // LANES):
            lanes = pl.ds(t * LANES, LANES)
            turned = z[group, t * LANES : (t + 1) * LANES, :].T
            for part in range(5 - group):
                d = 5 * group + part
                for s in range(3):
                    sets[s, d, :, lanes] = turned[24 * part + 8 * s : 24 * part + 8 * s + 8]
                base = 24 * part
                to_high[2 * d : 2 * d + 1, lanes] = turned[base : base + 1]
                to_high[2 * d + 1 : 2 * d + 2, lanes] = turned[base + 8 : base + 9]
                to_low[2 * d : 2 * d + 1, lanes] = turned[base + 15 : base + 16]
                to_low[2 * d + 1 : 2 * d + 2, lanes] = turned[base + 23 : base + 24]


def ghost_kernel(
    count_y,
    ids,
    coarse,
    low,
    high,
    sets,
    from_low,
    from_high,
    message,
    inject,
    first,
    last,
    turn,
    mt,
    old_t,
    post_t,
    new_t,
    g_t,
    pack_t,
    raw_r,
    post_r,
    new_r,
    g_r,
    pack_r,
    sems,
):
    blocks_x = coarse.shape[1]
    width = blocks_x * COARSE_EDGE
    wide = width + LANES
    tiles = wide // LANES
    width_y = LANES
    blocks_y = width_y // COARSE_EDGE
    total_y = width_y * count_y
    base_y = lax.axis_index("gy") * width_y
    copy_first = pltpu.make_async_copy(coarse.at[:, :, pl.ds(0, 8), :], first, sems.at[0])
    copy_last = pltpu.make_async_copy(
        coarse.at[:, :, pl.ds(COARSE_EDGE - 8, 8), :], last, sems.at[1]
    )
    copy_first.start()
    copy_last.start()

    turn[...] = jnp.full(turn.shape, 0.1, F32)
    for d in range(9):
        turn[4 * d : 4 * d + 2, :] = from_high[2 * d : 2 * d + 2, :]
        at = (4 * d - 2) % LANES
        turn[at : at + 2, :] = from_low[2 * d : 2 * d + 2, :]
    for t in range(tiles):
        mt[t * LANES : (t + 1) * LANES, :] = turn[:, t * LANES : (t + 1) * LANES].T
    tile = (8, LANES)
    row8 = row_of(tile)

    def collide_t(t, carry):
        lanes = pl.ds(pl.multiple_of(t * LANES, LANES), LANES)
        for s in range(3):
            p = []
            for d in range(9):
                value = sets[s, d, :, lanes]
                if s < 2:
                    value = jnp.where(row8 == 0, from_low[2 * d + s : 2 * d + s + 1, lanes], value)
                if s > 0:
                    value = jnp.where(
                        row8 == 7, from_high[2 * d + s - 1 : 2 * d + s, lanes], value
                    )
                if s == 1:
                    old_t[d, :, lanes] = value
                p.append(value)
            out = relax(p, COARSE)
            for d in range(9):
                post_t[s, d, :, lanes] = out[d]
        return carry

    lax.fori_loop(0, tiles, collide_t, 0)
    turn[...] = jnp.zeros(turn.shape, F32)
    row_t = row_of((8, wide))
    coord_t = base_y + 32 * (row_t & 3) + jnp.where(row_t < 4, -1, 32)
    for d in range(9):
        source = post_t[{1: 0, 0: 1, -1: 2}[along_y[d]], d]
        if along_x[d]:
            source = pltpu.roll(source, along_x[d] % wide, 1)
        back = coord_t - along_y[d]
        beyond = (back < 0) | (back >= total_y)
        new_t[d] = jnp.where(beyond, post_t[1, opposite[d]], source)
    for j in range(3):
        for side, (d, row) in enumerate(((LEFT[j], 0), (RIGHT[j], 7))):
            source = post_t[1, d]
            if along_x[d]:
                source = pltpu.roll(source, along_x[d] % wide, 1)
            turn[3 * side + j : 3 * side + j + 1, :] = source[row : row + 1, :]
    for t in range(width // LANES):
        inject[t * LANES : (t + 1) * LANES, :] = turn[:, t * LANES : (t + 1) * LANES].T

    def ghosts_t(t, carry):
        lanes = pl.ds(pl.multiple_of(t * LANES, LANES), LANES)
        old = [old_t[d, :, lanes] for d in range(9)]
        mean = [0.5 * (old[d] + new_t[d, :, lanes]) for d in range(9)]
        for sub, p in enumerate((old, mean)):
            out = relax(p, GHOST, LEFT + RIGHT)
            for j in range(3):
                g_t[sub, j, :, lanes] = jnp.where(row8 < 4, out[LEFT[j]], out[RIGHT[j]])
        return carry

    lax.fori_loop(0, tiles, ghosts_t, 0)
    lane8 = lane_of(tile)
    for sub in range(2):
        moved = [pltpu.roll(g_t[sub, j], 1, 1) for j in range(3)]
        for bx in range(blocks_x):
            t, off = divmod(COARSE_EDGE * bx, LANES)
            got = []
            for j in range(3):
                shift = (WINDOW * j - off) % LANES
                value = moved[j][:, t * LANES : (t + 1) * LANES]
                value = pltpu.roll(value, shift, 1) if shift else value
                if off == LANES - COARSE_EDGE:
                    after = moved[j][:, (t + 1) * LANES : (t + 2) * LANES]
                    after = pltpu.roll(after, shift, 1)
                    value = jnp.where(lane8 < WINDOW * j + COARSE_EDGE, value, after)
                got.append(value)
            pack_t[sub, bx] = jnp.where(
                lane8 < WINDOW, got[0], jnp.where(lane8 < 2 * WINDOW, got[1], got[2])
            )

    plane = (blocks_x, LANES)
    rows_b = row_of(plane)

    def lower(value, row):
        return jnp.where(rows_b == 0, row, pltpu.roll(value, 1, 0))

    def upper(value, row):
        return jnp.where(rows_b == blocks_x - 1, row, pltpu.roll(value, blocks_x - 1, 0))

    def every(ref, start, step):
        return ref[pl.ds(start, blocks_x, stride=step), :]

    side_rows = [every(mt, c, COARSE_EDGE) for c in (0, 1, COARSE_EDGE - 2, COARSE_EDGE - 1)]
    m0, m1, m30, m31 = side_rows
    extra = (
        lower(m30, mt[wide - 2 : wide - 1, :]),
        lower(m31, mt[wide - 1 : wide, :]),
        m0,
        m31,
        upper(m0, mt[width : width + 1, :]),
        upper(m1, mt[width + 1 : width + 2, :]),
    )
    copy_first.wait()
    copy_last.wait()
    first2 = first.reshape(9 * blocks_x * 8, LANES)
    last2 = last.reshape(9 * blocks_x * 8, LANES)
    for d in range(9):
        at = d * blocks_x * 8
        a0, a1 = every(first2, at, 8), every(first2, at + 1, 8)
        b30, b31 = every(last2, at + 6, 8), every(last2, at + 7, 8)
        main = (
            lower(b30, low[d, 0:1, :]),
            lower(b31, low[d, 1:2, :]),
            a0,
            b31,
            upper(a0, high[d, 0:1, :]),
            upper(a1, high[d, 1:2, :]),
        )
        for s in range(6):
            raw_r[s, d, :, 0:LANES] = main[s]
            value = extra[s]
            raw_r[s, d, :, LANES:] = pltpu.roll(value, (-4 * d) % LANES, 1) if d else value

    def collide_r(k, carry):
        rows = pl.ds(pl.multiple_of(k * 8, 8), 8)
        for s in range(6):
            for half in range(2):
                lanes = pl.ds(half * LANES, LANES)
                out = relax([raw_r[s, d, rows, lanes] for d in range(9)], COARSE)
                for d in range(9):
                    post_r[s, d, rows, lanes] = out[d]
        return carry

    lax.fori_loop(0, blocks_x // 8, collide_r, 0)
    double = (8, 2 * LANES)
    lane_r = lane_of(double)
    coord_r = base_y + jnp.where(lane_r < LANES + 2, lane_r, lane_r - 2 * LANES)

    def ghosts_r(k, carry):
        rows = pl.ds(pl.multiple_of(k * 8, 8), 8)
        for side in range(2):
            for d in range(9):
                source = post_r[3 * side + {1: 0, 0: 1, -1: 2}[along_x[d]], d, rows, :]
                if along_y[d]:
                    source = pltpu.roll(source, along_y[d] % (2 * LANES), 1)
                back = coord_r - along_y[d]
                beyond = (back < 0) | (back >= total_y)
                new_r[d] = jnp.where(beyond, post_r[3 * side + 1, opposite[d], rows, :], source)
            which = (UP, DOWN)[side]
            for half in range(2):
                lanes = pl.ds(half * LANES, LANES)
                old = [raw_r[3 * side + 1, d, rows, lanes] for d in range(9)]
                mean = [0.5 * (old[d] + new_r[d, :, lanes]) for d in range(9)]
                for sub, p in enumerate((old, mean)):
                    out = relax(p, GHOST, which)
                    for j in range(3):
                        g_r[j, sub, :, lanes] = out[which[j]]
            for sub in range(2):
                moved = [pltpu.roll(g_r[j, sub], 1, 1) for j in range(3)]
                for by in range(blocks_y):
                    got = []
                    for j in range(3):
                        off = COARSE_EDGE * by
                        shift = (WINDOW * j - off) % LANES
                        value = moved[j][:, 0:LANES]
                        value = pltpu.roll(value, shift, 1) if shift else value
                        if off == LANES - COARSE_EDGE:
                            after = pltpu.roll(moved[j][:, LANES:], shift, 1)
                            value = jnp.where(lane8 < WINDOW * j + COARSE_EDGE, value, after)
                        got.append(value)
                    pack_r[side, sub, by, rows, :] = jnp.where(
                        lane8 < WINDOW, got[0], jnp.where(lane8 < 2 * WINDOW, got[1], got[2])
                    )
        return carry

    lax.fori_loop(0, blocks_x // 8, ghosts_r, 0)

    def pick(q, carry):
        block = jnp.maximum(ids[q], 0)
        bx = lax.div(block, blocks_y)
        by = block - bx * blocks_y
        for sub in range(2):
            for side in range(2):
                row = 4 * sub + side
                message[q, row : row + 1, :] = pack_r[side, sub, by, pl.ds(bx, 1), :]
                row = 4 * sub + 2 + side
                message[q, row : row + 1, :] = pack_t[sub, bx, pl.ds(4 * side + by, 1), :]
        return carry

    lax.fori_loop(0, message.shape[0], pick, 0)


def start_kernel(slot, fine, post, sem):
    places = post.shape[1]
    copies = []
    for q in range(places):
        source = fine.at[:, pl.ds(jnp.maximum(slot[q], 0), 1), :]
        copy = pltpu.make_async_copy(source, post.at[:, pl.ds(q, 1), :], sem.at[q])
        copy.start()
        copies.append(copy)
    for copy in copies:
        copy.wait()

    def body(k, carry):
        lanes = pl.ds(pl.multiple_of(k * LANES, LANES), LANES)
        for h in range(places // 8):
            rows = pl.ds(8 * h, 8)
            out = relax([post[d, rows, lanes] for d in range(9)], FINE)
            for d in range(9):
                post[d, rows, lanes] = out[d]
        return carry

    lax.fori_loop(0, post.shape[2] // LANES, body, 0, unroll=2)


def fine_kernel(slot, post, ghosts, result, back, post_two, mean, line):
    places = post.shape[1]
    tiles = post.shape[2] // LANES
    tile = (8, LANES)
    lane, row = lane_of(tile), row_of(tile)
    low_half = lane < 64
    at_low = (lane & 63) == 0
    at_high = (lane & 63) == 63
    odd = (lane & 1) == 1
    ghosts2 = ghosts.reshape(places * 8, LANES)
    over = [WINDOW * j + 1 + (((lane & 63) - c) >> 1) for j, c in enumerate(ORDER)]
    cell = 2 * (lane & 63) + (lane >> 6)
    along = [(WINDOW * j + 1 + ((cell - c) >> 1)) & (LANES - 1) for j, c in enumerate(ORDER)]
    squeeze = 64 * ((lane >> 5) & 1) + 2 * (lane & 31) + (lane >> 6)

    def half(h, carry):
        rows = pl.ds(pl.multiple_of(8 * h, 8), 8)
        wall = jnp.zeros(tile, jnp.int32)
        for r in range(8):
            wall = jnp.where(row == r, slot[places + 8 * h + r], wall)
        wall_low = at_low & ((wall & 1) != 0)
        wall_high = at_high & ((wall & 2) != 0)

        def substep(sub, source, emit):
            border = [
                ghosts2[pl.ds(h * 64 + 4 * sub + side, 8, stride=8), :] for side in range(4)
            ]
            up = [take_lanes(border[0], over[j]) for j in range(3)]
            down = [take_lanes(border[1], over[j]) for j in range(3)]
            left = [take_lanes(border[2], along[j]) for j in range(3)]
            right = [take_lanes(border[3], along[j]) for j in range(3)]

            def load(d, k):
                return source[d, rows, k * LANES : (k + 1) * LANES]

            def crossed(d, k):
                if k < 0:
                    return up[UP.index(d)]
                if k == tiles:
                    return down[DOWN.index(d)]
                return pltpu.roll(load(d, k), (64 + along_y[d]) % LANES, 1)

            before = {d: crossed(d, -1) for d in UP}
            now = {d: crossed(d, 0) for d in DOWN}
            for k in range(tiles):
                out = []
                for d in range(9):
                    if along_x[d] > 0:
                        turned = crossed(d, k)
                        value = jnp.where(low_half, before[d], turned)
                        before[d] = turned
                    elif along_x[d] < 0:
                        turned = crossed(d, k + 1)
                        value = jnp.where(low_half, now[d], turned)
                        now[d] = turned
                    else:
                        value = load(d, k)
                        if along_y[d]:
                            value = pltpu.roll(value, along_y[d] % LANES, 1)
                    if along_y[d] > 0:
                        ghost = left[LEFT.index(d)]
                        ghost = pltpu.roll(ghost, (-k) % LANES, 1) if k else ghost
                        value = jnp.where(at_low, ghost, value)
                        value = jnp.where(wall_low, load(opposite[d], k), value)
                    elif along_y[d] < 0:
                        ghost = pltpu.roll(right[RIGHT.index(d)], 63 - k, 1)
                        value = jnp.where(at_high, ghost, value)
                        value = jnp.where(wall_high, load(opposite[d], k), value)
                    out.append(value)
                emit(k, out)

        def emit_first(k, p):
            out = relax(p, FINE)
            for d in range(9):
                post_two[d, :, k * LANES : (k + 1) * LANES] = out[d]

        def emit_second(k, p):
            j, i = divmod(k, 8)
            total = []
            for d in range(9):
                result[d, rows, k * LANES : (k + 1) * LANES] = p[d]
                pair = p[d] + pltpu.roll(p[d], 64, 1)
                value = pair + pltpu.roll(pair, LANES - 1 if j < 2 else 1, 1)
                if j:
                    kept = mean[d, i]
                    side = low_half if j & 1 == 0 else ~low_half
                    value = jnp.where(side & odd if j > 1 else side, value, kept)
                if j < 3:
                    mean[d, i] = value
                total.append(value)
            if j == 3:
                out = relax([0.25 * value for value in total], COALESCE)
                for d in range(9):
                    line[d, i * 8 : i * 8 + 8, :] = take_lanes(out[d], squeeze)

        post_rows = post
        substep(0, post_rows, emit_first)
        substep(1, _Rows(post_two), emit_second)
        for d in range(9):
            flat = line.at[d]
            for q in range(8):
                back[8 * h + q, d * 8 : d * 8 + 8, :] = flat[pl.ds(q, 8, stride=8), :]
        return carry

    lax.fori_loop(0, places // 8, half, 0)


class _Rows:
    def __init__(self, ref):
        self.ref = ref

    def __getitem__(self, key):
        d, _, lanes = key
        return self.ref[d, :, lanes]


def store_kernel(slot, result, fine, sem):
    places = result.shape[1]

    def copy(q):
        target = fine.at[:, pl.ds(jnp.maximum(slot[q], 0), 1), :]
        return pltpu.make_async_copy(result.at[:, pl.ds(q, 1), :], target, sem.at[q])

    for q in range(places):

        @pl.when(slot[q] >= 0)
        def _(q=q):
            copy(q).start()

    for q in range(places):

        @pl.when(slot[q] >= 0)
        def _(q=q):
            copy(q).wait()


def coarse_kernel(count_y, coarse, low, high, inject, after, new, post, sems):
    width = coarse.shape[1]
    tile = (8, LANES)
    lane = lane_of(tile)
    copies = [
        pltpu.make_async_copy(coarse.at[d], post.at[d, pl.ds(8, width), :], sems.at[d])
        for d in range(9)
    ]
    for copy in copies:
        copy.start()
    out = relax([low[d, 1:2, :] for d in range(9)], COARSE)
    for d in range(9):
        post[d, 7:8, :] = out[d]
    out = relax([high[d, 0:1, :] for d in range(9)], COARSE)
    for d in range(9):
        post[d, width + 8 : width + 9, :] = out[d]
    for copy in copies:
        copy.wait()

    def collide(k, carry):
        rows = pl.ds(pl.multiple_of(8 + 8 * k, 8), 8)
        out = relax([post[d, rows, :] for d in range(9)], COARSE)
        for d in range(9):
            post[d, rows, :] = out[d]
        return carry

    lax.fori_loop(0, width // 8, collide, 0, unroll=4)
    index_y = lax.axis_index("gy")
    wall_low = (lane == 0) & (index_y == 0)
    wall_high = (lane == LANES - 1) & (index_y == count_y - 1)

    def stream(k, carry):
        start = pl.multiple_of(8 * k, 8)
        edge = inject[pl.ds(start, 8), :]
        for d in range(9):
            value = post[d, pl.ds(start + (8 - along_x[d]), 8), :]
            if along_y[d]:
                value = pltpu.roll(value, along_y[d] % LANES, 1)
                same = post[opposite[d], pl.ds(start + 8, 8), :]
                if along_y[d] > 0:
                    j = LEFT.index(d)
                    value = jnp.where(lane == 0, pltpu.roll(edge, (-j) % LANES, 1), value)
                    value = jnp.where(wall_low, same, value)
                else:
                    j = RIGHT.index(d)
                    moved = pltpu.roll(edge, LANES - 4 - j, 1)
                    value = jnp.where(lane == LANES - 1, moved, value)
                    value = jnp.where(wall_high, same, value)
            new[d, pl.ds(start, 8), :] = value
        return carry

    lax.fori_loop(0, width // 8, stream, 0, unroll=4)


def patch_kernel(blocks_y, ids, new, back, out, buf, sems):
    width = new.shape[1]
    load = pltpu.make_async_copy(new, buf, sems.at[0])
    load.start()
    lane = lane_of((8, LANES))
    load.wait()

    def patch(q, carry):
        block = ids[q]

        @pl.when(block >= 0)
        def _():
            bx = lax.div(block, blocks_y)
            by = block - bx * blocks_y
            inside = (lane >> 5) == by
            for d in range(9):
                value = back[q, d * 8 : d * 8 + 8, :]
                for j in range(4):
                    rows = pl.ds(pl.multiple_of(COARSE_EDGE * bx + 8 * j, 8), 8)
                    moved = pltpu.roll(value, lax.rem(by + 4 - j, 4) * 32, 1)
                    buf[d, rows, :] = jnp.where(inside, moved, buf[d, rows, :])

        return carry

    lax.fori_loop(0, ids.shape[0], patch, 0)
    store = pltpu.make_async_copy(buf, out, sems.at[1])
    store.start()
    store.wait()


def local(coarse_pop, fine_pop, fine_block):
    width_x, width_y = coarse_pop.shape[1:]
    blocks_x = width_x // COARSE_EDGE
    blocks_y = width_y // COARSE_EDGE
    count_x = lax.axis_size("gx")
    count_y = lax.axis_size("gy")
    columns = blocks_y * count_y
    places = count_x * CAP
    slots = fine_block.shape[0]
    cells = FINE_EDGE * FINE_EDGE
    wide = width_x + LANES
    smem = pl.BlockSpec(memory_space=pltpu.SMEM)
    vmem = pl.BlockSpec(memory_space=pltpu.VMEM)
    hbm = pl.BlockSpec(memory_space=pl.ANY)
    sds = jax.ShapeDtypeStruct
    forward = [(i, (i + 1) % count_x) for i in range(count_x)]
    backward = [(target, source) for source, target in forward]
    low = lax.ppermute(coarse_pop[:, width_x - 2 :, :], "gx", forward)
    high = lax.ppermute(coarse_pop[:, :2, :], "gx", backward)
    ids, slot = pl.pallas_call(
        functools.partial(table_kernel, columns, blocks_x, blocks_y, count_x),
        out_shape=(sds((places,), jnp.int32), sds((2 * places,), jnp.int32)),
        in_specs=[smem],
        out_specs=(smem, smem),
        scratch_shapes=[pltpu.SMEM((count_x,), jnp.int32)],
        name="table",
    )(fine_block)
    wanted = lax.all_to_all(ids, "gx", split_axis=0, concat_axis=0, tiled=True)
    sets, to_high, to_low = pl.pallas_call(
        pack_kernel,
        out_shape=(sds((3, 9, 8, wide), F32), sds((24, wide), F32), sds((24, wide), F32)),
        in_specs=[hbm, vmem, vmem],
        out_specs=(vmem, vmem, vmem),
        scratch_shapes=[
            pltpu.VMEM((9, width_x, LANES), F32),
            pltpu.VMEM((2, 9, 8, LANES), F32),
            pltpu.VMEM((2, wide, LANES), F32),
            pltpu.SemaphoreType.DMA((9,)),
        ],
        name="pack",
    )(coarse_pop, low, high)
    forward_y = [(i, (i + 1) % count_y) for i in range(count_y)]
    backward_y = [(target, source) for source, target in forward_y]
    from_low = lax.ppermute(to_high, "gy", forward_y)
    from_high = lax.ppermute(to_low, "gy", backward_y)
    fine_turned = jnp.transpose(fine_pop, (1, 0, 2))
    post = pl.pallas_call(
        start_kernel,
        out_shape=sds((9, places, cells), F32),
        in_specs=[smem, hbm],
        out_specs=vmem,
        scratch_shapes=[pltpu.SemaphoreType.DMA((places,))],
        name="start",
    )(slot, fine_turned)
    message, inject = pl.pallas_call(
        functools.partial(ghost_kernel, count_y),
        out_shape=(sds((places, 8, LANES), F32), sds((width_x, LANES), F32)),
        in_specs=[smem, hbm, vmem, vmem, vmem, vmem, vmem],
        out_specs=(vmem, vmem),
        scratch_shapes=[
            pltpu.VMEM((9, blocks_x, 8, LANES), F32),
            pltpu.VMEM((9, blocks_x, 8, LANES), F32),
            pltpu.VMEM((LANES, wide), F32),
            pltpu.VMEM((wide, LANES), F32),
            pltpu.VMEM((9, 8, wide), F32),
            pltpu.VMEM((3, 9, 8, wide), F32),
            pltpu.VMEM((9, 8, wide), F32),
            pltpu.VMEM((2, 3, 8, wide), F32),
            pltpu.VMEM((2, blocks_x, 8, LANES), F32),
            pltpu.VMEM((6, 9, blocks_x, 2 * LANES), F32),
            pltpu.VMEM((6, 9, blocks_x, 2 * LANES), F32),
            pltpu.VMEM((9, 8, 2 * LANES), F32),
            pltpu.VMEM((3, 2, 8, 2 * LANES), F32),
            pltpu.VMEM((2, 2, blocks_y, blocks_x, LANES), F32),
            pltpu.SemaphoreType.DMA((2,)),
        ],
        name="ghost",
    )(
        wanted,
        coarse_pop.reshape(9, blocks_x, COARSE_EDGE, width_y),
        low,
        high,
        sets,
        from_low,
        from_high,
    )
    ghosts = lax.all_to_all(message, "gx", split_axis=0, concat_axis=0, tiled=True)
    result, back = pl.pallas_call(
        fine_kernel,
        out_shape=(sds((9, places, cells), F32), sds((places, 72, LANES), F32)),
        in_specs=[smem, vmem, vmem],
        out_specs=(vmem, vmem),
        scratch_shapes=[
            pltpu.VMEM((9, 8, cells), F32),
            pltpu.VMEM((9, 8, 8, LANES), F32),
            pltpu.VMEM((9, 64, LANES), F32),
        ],
        name="fine",
    )(slot, post, ghosts)
    returned = lax.all_to_all(back, "gx", split_axis=0, concat_axis=0, tiled=True)
    fine_out = pl.pallas_call(
        store_kernel,
        out_shape=sds((9, slots, cells), F32),
        in_specs=[smem, vmem],
        out_specs=hbm,
        scratch_shapes=[pltpu.SemaphoreType.DMA((places,))],
        name="store",
    )(slot, result)
    new = pl.pallas_call(
        functools.partial(coarse_kernel, count_y),
        out_shape=sds((9, width_x, width_y), F32),
        in_specs=[hbm, vmem, vmem, vmem, hbm],
        out_specs=vmem,
        scratch_shapes=[
            pltpu.VMEM((9, width_x + 16, LANES), F32),
            pltpu.SemaphoreType.DMA((9,)),
        ],
        name="coarse",
    )(coarse_pop, low, high, inject, back)
    coarse_out = pl.pallas_call(
        functools.partial(patch_kernel, blocks_y),
        out_shape=sds((9, width_x, width_y), F32),
        in_specs=[smem, hbm, vmem],
        out_specs=hbm,
        scratch_shapes=[
            pltpu.VMEM((9, width_x, LANES), F32),
            pltpu.SemaphoreType.DMA((2,)),
        ],
        name="patch",
    )(wanted, new, returned)
    return (coarse_out, jnp.transpose(fine_out, (1, 0, 2)))


def solution(mesh):
    return jax.shard_map(
        local,
        mesh=mesh,
        in_specs=(P(None, "gx", "gy"), P(("gx", "gy"), None, None), P(("gx", "gy"))),
        out_specs=(P(None, "gx", "gy"), P(("gx", "gy"), None, None)),
        check_vma=False,
    )
```

time: 649 us -> 104 us (0.16); the launches traced: 638 us -> 103 us
  local copies, waits for them, and re-layouts: 472 us -> 5.43 us
  other arithmetic: 89.7 us -> 0.64 us
  Pallas kernels: 0 us -> 63.5 us
  matrix products: 33.3 us -> 0 us
    gather x129 -> x0, local copies, waits for them, and re-layouts: 113 us -> none
    reshape x18 -> x0, local copies, waits for them, and re-layouts: 109 us -> none  [the longest x2 28.3 us: local(): coarse_next.reshape(9, blocks_x, COARSE_EDGE, blocks_y, COARSE_EDGE)]
    unnamed x129 -> x12, local copies, waits for them, and re-layouts: 90.3 us -> 2.72 us
    pallas_call x0 -> x8, Pallas kernels: none -> 63.5 us  [the longest x1 14.8 us: local(): pl.pallas_call(fine_kernel, out_shape=(sds((9, places, cells), F32), sds(...]
    another operation x30 -> x0, local copies, waits for them, and re-layouts: 52.2 us -> none  [the longest x21 26.6 us: fine_substep(): return jnp.stack(result, axis=1)]
    reduce_sum x10 -> x0, other arithmetic: 46.6 us -> none  [the longest x1 19.8 us: coalesce(): average = jnp.sum(grouped, axis=(3, 5)) * 0.25]
    slice x32 -> x1, local copies, waits for them, and re-layouts: 45.7 us -> 0.8 us  [local(): high = lax.ppermute(coarse_pop[:, :2, :], 'gx', backward)]
    dot_general x5 -> x0, matrix products: 33.3 us -> none  [collide(): jnp.einsum('ij,...jn->...in', matrix, popul - balance, precision=lax.Prec...]
  transfers between devices with their start and end apart: 6 -> 6, of which waited for: 3 -> 4; matrix products, arithmetic and copies ran while one was open for 15% -> 1% of each run, Pallas kernels for 0% -> 20%
where the time goes in v1:
time: 104 us; the launch traced here: 103 us
  Pallas kernels  63.5 us (61%)
  starting transfers between devices  15.3 us (15%)
  blocking collectives  8.85 us (9%)
  waiting for transfers between devices  8.62 us (8%)
  local copies, waits for them, and re-layouts  5.43 us (5%)
    pallas_call x1, Pallas kernels, local(): pl.pallas_call(fine_kernel, out_shape=(sds((9, places, cells), F32), sds(...  14.8 us
    pallas_call x1, Pallas kernels, local(): pl.pallas_call(pack_kernel, out_shape=(sds((3, 9, 8, wide), F32), sds((24...  14.4 us
    pallas_call x1, Pallas kernels, local(): pl.pallas_call(functools.partial(coarse_kernel, count_y), out_shape=sds((...  10.9 us
    all_to_all x1, blocking collectives, local(): wanted = lax.all_to_all(ids, 'gx', split_axis=0, concat_axis=0, tiled=True)  8.85 us
    pallas_call x1, Pallas kernels, local(): pl.pallas_call(functools.partial(patch_kernel, blocks_y), out_shape=sds((...  7.53 us
    pallas_call x1, Pallas kernels, local(): pl.pallas_call(functools.partial(ghost_kernel, count_y), out_shape=(sds((...  6.21 us
    ppermute x1, starting transfers between devices, local(): high = lax.ppermute(coarse_pop[:, :2, :], 'gx', backward)  6.05 us
    ppermute x1, waiting for transfers between devices, local(): low = lax.ppermute(coarse_pop[:, width_x - 2:, :], 'gx', forward)  4.98 us
  transfers between devices with their start and end apart: 6, of which 4 were waited for; matrix products, arithmetic and copies ran while one was open for 1% of the time, Pallas kernels for 20%

profile of v1, /device:TPU:0, one launch (start us, length us, event | category | flops | bytes accessed | tf_op | source)
XLA Modules:
  0.0 103.0 jit_solution(14748349236773520509)
XLA Ops:
  0.6 0.8 fusion
  1.4 6.0 %collective-permute-start.1 = (f32[9,2,128]{2,1,0:T(2,128)S(1)}, f32[9,2,128]{2,1,0:T(2,128)S(1)}, u32[]{:S(2)}, u32[]{:S(2)}) collective-permute-start(f32[9,2,128]{2,1,0:T(2,128)S(1)} %get-tuple-element.20), channel_id=1, source_target_pairs={{4,0},{8,4},{12,8},{16,12},{20,16},{24,20},{28,24},{0,28},{5,1},{9... | collective-permute-start | bytes 27656 | tf_op jit(solution)/shard_map/ppermute | solution.py:667
  7.5 0.0 collective-permute-start
  7.5 1.4 %collective-permute-done.1.high = f32[9,2,128]{2,1,0:T(2,128)S(1)} collective-permute-done((f32[9,2,128]{2,1,0:T(2,128)S(1)}, f32[9,2,128]{2,1,0:T(2,128)S(1)}, u32[]{:S(2)}, u32[]{:S(2)}) %collective-permute-start.1) | collective-permute-done | bytes 9248 | tf_op jit(solution)/shard_map/ppermute | solution.py:667
  8.9 0.0 copy-start.4
  8.9 5.0 %collective-permute-done.low = f32[9,2,128]{2,1,0:T(2,128)S(1)} collective-permute-done((f32[9,2,128]{2,1,0:T(2,128)S(1)}, f32[9,2,128]{2,1,0:T(2,128)S(1)}, u32[]{:S(2)}, u32[]{:S(2)}) %collective-permute-start) | collective-permute-done | bytes 9248 | tf_op jit(solution)/shard_map/ppermute | solution.py:666
  13.8 0.0 copy-done.4
  13.8 0.0 copy-start.5
  13.8 0.6 copy-done.5
  14.4 14.4 %pack.1 = (f32[3,9,8,1152]{3,2,1,0:T(8,128)}, f32[24,1152]{1,0:T(8,128)}, f32[24,1152]{1,0:T(8,128)}) custom-call(f32[9,1024,128]{2,1,0:T(8,128)} %coarse.5, f32[9,2,128]{2,1,0:T(2,128)} %copy-done.5, f32[9,2,128]{2,1,0:T(2,128)} %copy-done.4), custom_call_target="tpu_custom_call" | custom-call | tf_op jit(solution)/shard_map/pack/pallas_call | solution.py:677
  28.8 0.1 collective-permute-start.2
  28.9 1.7 %collective-permute-start.3 = (f32[24,1152]{1,0:T(8,128)}, f32[24,1152]{1,0:T(8,128)S(1)}, u32[]{:S(2)}, u32[]{:S(2)}) collective-permute-start(f32[24,1152]{1,0:T(8,128)} %get-tuple-element.14), channel_id=1, source_target_pairs={{1,0},{2,1},{3,2},{0,3},{5,4},{6,5},{7,6},{4,7},{9,8},{10,9},{11,1... | collective-permute-start | bytes 331784 | tf_op jit(solution)/shard_map/ppermute | solution.py:693
  30.6 1.4 %table.1 = (s32[16]{0:T(128)}, s32[32]{0:T(128)}) custom-call(s32[16]{0:T(128)} %block_ref.1), custom_call_target="tpu_custom_call" | custom-call | tf_op jit(solution)/shard_map/table/pallas_call | solution.py:668
  32.0 0.7 all_to_all.13
  32.8 8.9 %all_to_all.21 = s32[8,2,1]{1,2,0:T(1,128)S(1)} all-to-all(s32[8,2,1]{1,2,0:T(1,128)S(1)} %bitcast.8), channel_id=1, replica_groups=mesh['gx'=8,'gy'=4] {'gx'}, dimensions={0} | all-to-all | bytes 128 | tf_op jit(solution)/shard_map/all_to_all | solution.py:676
  41.6 0.6 broadcast.3
  42.2 0.6 reduce.3
  42.9 0.6 all_to_all.15.ids
  43.5 0.0 collective-permute-done.2.from_low
  43.5 0.0 copy-start.2
  43.5 0.0 collective-permute-done.3.from_high
  43.5 0.0 copy-start.3
  43.5 0.6 copy-done.2
  44.1 0.0 copy-done.3
  44.2 6.2 %ghost.1 = (f32[16,8,128]{2,1,0:T(8,128)}, f32[1024,128]{1,0:T(8,128)}) custom-call(s32[16]{0:T(128)} %all_to_all.15.ids, f32[9,32,32,128]{3,2,1,0:T(8,128)} %bitcast.5, f32[9,2,128]{2,1,0:T(2,128)} %copy-done.5, f32[9,2,128]{2,1,0:T(2,128)} %copy-done.4, f32[3,9,8,1152]{3,2,1,0:T(8,128)} %get-tuple-element.12.sets, f32[24,1152]{1,0:T(8,128)} %copy-done.2, ...), custom_call_target="tpu_custom_call" | custom-call | tf_op jit(solution)/shard_map/ghost/pallas_call | solution.py:703
  50.4 3.4 %all-to-all-start.1 = ((f32[16,8,128]{2,1,0:T(8,128)}), f32[16,8,128]{2,1,0:T(8,128)S(1)}, u32[]{:S(2)}, u32[]{:S(2)}) async-start(f32[16,8,128]{2,1,0:T(8,128)} %get-tuple-element.17), calls=%async_computation.1 | async-start | bytes 131072 | tf_op jit(solution)/shard_map/all_to_all | solution.py:735
  53.7 5.0 %start.1.post = f32[9,16,4096]{2,1,0:T(8,128)} custom-call(s32[32]{0:T(128)} %get-tuple-element.16.slot, f32[9,16,4096]{2,1,0:T(8,128)} %bitcast.6), custom_call_target="tpu_custom_call" | custom-call | tf_op jit(solution)/shard_map/start/pallas_call | solution.py:695
  58.7 1.9 %all-to-all-done.1.ghosts = f32[16,8,128]{2,1,0:T(8,128)S(1)} async-done(((f32[16,8,128]{2,1,0:T(8,128)}), f32[16,8,128]{2,1,0:T(8,128)S(1)}, u32[]{:S(2)}, u32[]{:S(2)}) %all-to-all-start.1) | async-done | bytes 65568 | tf_op jit(solution)/shard_map/all_to_all | solution.py:735
  60.6 0.0 copy-start.1
  60.6 0.6 copy-done.1
  61.2 14.8 %fine.1 = (f32[9,16,4096]{2,1,0:T(8,128)}, f32[16,72,128]{2,1,0:T(8,128)}) custom-call(s32[32]{0:T(128)} %get-tuple-element.16.slot, f32[9,16,4096]{2,1,0:T(8,128)} %start.1.post, f32[16,8,128]{2,1,0:T(8,128)} %copy-done.1), custom_call_target="tpu_custom_call" | custom-call | tf_op jit(solution)/shard_map/fine/pallas_call | solution.py:736
  76.1 4.1 %all-to-all-start.2 = ((f32[16,72,128]{2,1,0:T(8,128)}), f32[16,72,128]{2,1,0:T(8,128)S(1)}, u32[]{:S(2)}, u32[]{:S(2)}) async-start(f32[16,72,128]{2,1,0:T(8,128)} %get-tuple-element.18.after), calls=%async_computation.2 | async-start | bytes 1179648 | tf_op jit(solution)/shard_map/all_to_all | solution.py:748
  80.1 3.2 %store.1 = f32[9,16,4096]{2,1,0:T(8,128)} custom-call(s32[32]{0:T(128)} %get-tuple-element.16.slot, f32[9,16,4096]{2,1,0:T(8,128)} %get-tuple-element.19.result), custom_call_target="tpu_custom_call" | custom-call | tf_op jit(solution)/shard_map/store/pallas_call | solution.py:749
  83.4 10.9 %coarse.4.new = f32[9,1024,128]{2,1,0:T(8,128)} custom-call(f32[9,1024,128]{2,1,0:T(8,128)} %coarse.5, f32[9,2,128]{2,1,0:T(2,128)} %copy-done.5, f32[9,2,128]{2,1,0:T(2,128)} %copy-done.4, f32[1024,128]{1,0:T(8,128)} %get-tuple-element.15.inject, f32[16,72,128]{2,1,0:T(8,128)} %get-tuple-element.18.after), custom_call_target="tpu_custom_call" | custom-call | tf_op jit(solution)/shard_map/coarse/pallas_call | solution.py:757
  94.3 0.4 all-to-all-done.2.back
  94.7 0.0 copy-start
  94.7 0.8 copy-done
  95.5 7.5 %patch.1 = f32[9,1024,128]{2,1,0:T(8,128)} custom-call(s32[16]{0:T(128)} %all_to_all.15.ids, f32[9,1024,128]{2,1,0:T(8,128)} %coarse.4.new, f32[16,72,128]{2,1,0:T(8,128)} %copy-done), custom_call_target="tpu_custom_call" | custom-call | tf_op jit(solution)/shard_map/patch/pallas_call | solution.py:768
Async XLA Ops:
  1.4 7.4 %collective-permute-start.1 = (f32[9,2,128]{2,1,0:T(2,128)S(1)}, f32[9,2,128]{2,1,0:T(2,128)S(1)}, u32[]{:S(2)}, u32[]{:S(2)}) collective-permute-start(f32[9,2,128]{2,1,0:T(2,128)S(1)} %get-tuple-element.20), channel_id=1, source_target_pairs={{4,0},{8,4},{12,8},{16,12},{20,16},{24,20},{28,24},{0,28},{5,1},{9... | collective-permute-start | bytes 27656 | tf_op jit(solution)/shard_map/ppermute | solution.py:667
  7.5 6.4 %collective-permute-start = (f32[9,2,128]{2,1,0:T(2,128)S(1)}, f32[9,2,128]{2,1,0:T(2,128)S(1)}, u32[]{:S(2)}, u32[]{:S(2)}) collective-permute-start(f32[9,2,128]{2,1,0:T(2,128)S(1)} %get-tuple-element.21), channel_id=1, source_target_pairs={{0,4},{4,8},{8,12},{12,16},{16,20},{20,24},{24,28},{28,0},{1,5},{5... | collective-permute-start | bytes 27656 | tf_op jit(solution)/shard_map/ppermute | solution.py:666
  8.9 5.0 %copy-start.4 = (f32[9,2,128]{2,1,0:T(2,128)}, f32[9,2,128]{2,1,0:T(2,128)S(1)}, u32[]{:S(2)}) copy-start(f32[9,2,128]{2,1,0:T(2,128)S(1)} %collective-permute-done.1.high) | copy-start | bytes 27652
  13.8 0.6 copy-start.5
  28.8 14.6 %collective-permute-start.2 = (f32[24,1152]{1,0:T(8,128)}, f32[24,1152]{1,0:T(8,128)S(1)}, u32[]{:S(2)}, u32[]{:S(2)}) collective-permute-start(f32[24,1152]{1,0:T(8,128)} %get-tuple-element.13), channel_id=1, source_target_pairs={{0,1},{1,2},{2,3},{3,0},{4,5},{5,6},{6,7},{7,4},{8,9},{9,10},{10,1... | collective-permute-start | bytes 331784 | tf_op jit(solution)/shard_map/ppermute | solution.py:692
  28.9 14.6 %collective-permute-start.3 = (f32[24,1152]{1,0:T(8,128)}, f32[24,1152]{1,0:T(8,128)S(1)}, u32[]{:S(2)}, u32[]{:S(2)}) collective-permute-start(f32[24,1152]{1,0:T(8,128)} %get-tuple-element.14), channel_id=1, source_target_pairs={{1,0},{2,1},{3,2},{0,3},{5,4},{6,5},{7,6},{4,7},{9,8},{10,9},{11,1... | collective-permute-start | bytes 331784 | tf_op jit(solution)/shard_map/ppermute | solution.py:693
  43.5 0.6 copy-start.2
  43.5 0.7 copy-start.3
  50.4 10.2 %all-to-all-start.1 = ((f32[16,8,128]{2,1,0:T(8,128)}), f32[16,8,128]{2,1,0:T(8,128)S(1)}, u32[]{:S(2)}, u32[]{:S(2)}) async-start(f32[16,8,128]{2,1,0:T(8,128)} %get-tuple-element.17), calls=%async_computation.1 | async-start | bytes 131072 | tf_op jit(solution)/shard_map/all_to_all | solution.py:735
  60.6 0.6 copy-start.1
  76.1 18.6 %all-to-all-start.2 = ((f32[16,72,128]{2,1,0:T(8,128)}), f32[16,72,128]{2,1,0:T(8,128)S(1)}, u32[]{:S(2)}, u32[]{:S(2)}) async-start(f32[16,72,128]{2,1,0:T(8,128)} %get-tuple-element.18.after), calls=%async_computation.2 | async-start | bytes 1179648 | tf_op jit(solution)/shard_map/all_to_all | solution.py:748
  94.7 0.8 copy-start

commit v2 on v1

v2 whole, which is shorter than its diff:
```python
import functools

import jax
import jax.numpy as jnp
from jax import lax
from jax.experimental import pallas as pl
from jax.experimental.pallas import tpu as pltpu
from jax.sharding import PartitionSpec as P

FINE_EDGE = 64
COARSE_EDGE = 32
CAP = 2
LANES = 128
WINDOW = 42

along_x = [0, 1, 0, -1, 0, 1, -1, -1, 1]
along_y = [0, 0, 1, 0, -1, 1, 1, -1, -1]
opposite = [0, 3, 4, 1, 2, 7, 8, 5, 6]
UP = (1, 5, 8)
DOWN = (3, 6, 7)
LEFT = (2, 5, 6)
RIGHT = (4, 8, 7)
ORDER = (0, 1, -1)

F32 = jnp.float32
GRANT = pltpu.CompilerParams(vmem_limit_bytes=24 << 20)


def rates_of(relax_time, factor=1.0):
    return tuple((1.0 - factor) + factor * rate for rate in (1.4, 1.4, 1.2, 1.0 / relax_time))


COARSE = rates_of(0.65)
FINE = rates_of(0.8)
GHOST = rates_of(0.8, 0.8 / 1.3)
COALESCE = (1.0 - 1.3 / 0.8,) * 4


def relax(p, rates, which=tuple(range(9))):
    s_e, s_p, s_q, s_n = rates
    p0, p1, p2, p3, p4, p5, p6, p7, p8 = p
    s1, d1 = p1 + p3, p1 - p3
    s2, d2 = p2 + p4, p2 - p4
    s5, d5 = p5 + p7, p5 - p7
    s6, d6 = p6 + p8, p6 - p8
    axial, diagonal = s1 + s2, s5 + s6
    rho = p0 + axial + diagonal
    dq, sq = d5 - d6, d5 + d6
    jx, jy = d1 + dq, d2 + sq
    inv = 1.0 / rho
    xx, yy = jx * jx, jy * jy
    square = 3.0 * ((xx + yy) * inv)
    e = (axial - 2.0 * p0) + 4.0 * diagonal - square
    eps = 3.0 * (p0 - axial) + square
    a = (s_e / 36.0) * e
    b = (s_p / 36.0) * eps
    c = (s_q / 12.0) * (2.0 * dq - d1)
    d = (s_q / 12.0) * (2.0 * sq - d2)
    f = (s_n / 4.0) * ((s1 - s2) - (xx - yy) * inv)
    g = (s_n / 4.0) * ((s5 - s6) - (jx * jy) * inv)
    out = {}
    t = a + 2.0 * b
    w = 2.0 * a + b
    if 0 in which:
        out[0] = p0 + 4.0 * (a - b)
    if 1 in which:
        out[1] = p1 + ((t - f) + 2.0 * c)
    if 3 in which:
        out[3] = p3 + ((t - f) - 2.0 * c)
    if 2 in which:
        out[2] = p2 + ((t + f) + 2.0 * d)
    if 4 in which:
        out[4] = p4 + ((t + f) - 2.0 * d)
    if 5 in which:
        out[5] = p5 - ((w + g) + (c + d))
    if 7 in which:
        out[7] = p7 - ((w + g) - (c + d))
    if 6 in which:
        out[6] = p6 - ((w - g) - (c - d))
    if 8 in which:
        out[8] = p8 - ((w - g) + (c - d))
    return out


def lane_of(shape):
    return lax.broadcasted_iota(jnp.int32, shape, 1)


def row_of(shape):
    return lax.broadcasted_iota(jnp.int32, shape, 0)


def take_lanes(value, index):
    return jnp.take_along_axis(value, index, axis=1, mode="promise_in_bounds")


def ask_kernel(
    columns, blocks_x, blocks_y, count_x, block_hbm, coarse, ask, slot_ref, block_ref, id_ref, seen_ref, edge, rows, sems
):
    width = coarse.shape[1]
    places = count_x * CAP
    copies = [
        pltpu.make_async_copy(coarse.at[:, pl.ds(at, 8), :], edge.at[k], sems.at[k])
        for k, at in enumerate((0, width - 8))
    ]
    blocks = pltpu.make_async_copy(block_hbm, block_ref, sems.at[2])
    blocks.start()
    for copy in copies:
        copy.start()
    for place in range(places):
        id_ref[place] = -1
        slot_ref[place] = -1
        slot_ref[places + place] = 0
    for owner in range(count_x):
        seen_ref[owner] = 0
    blocks.wait()
    for slot in range(block_ref.shape[0]):
        block = block_ref[slot]
        column = lax.div(block, columns)
        row = block - column * columns
        owner = lax.div(column, blocks_x)
        rank = seen_ref[owner]
        seen_ref[owner] = rank + 1
        place = owner * CAP + rank
        id_ref[place] = (column - owner * blocks_x) * blocks_y + lax.rem(row, blocks_y)
        slot_ref[place] = slot
        slot_ref[places + place] = jnp.where(row == 0, 1, 0) + jnp.where(row == columns - 1, 2, 0)
    rows[...] = jnp.full(rows.shape, 0.1, F32)
    for copy in copies:
        copy.wait()
    for d in range(9):
        rows[0, 2 * d : 2 * d + 2, :] = edge[0, d, 0:2, :]
        rows[1, 2 * d : 2 * d + 2, :] = edge[1, d, 6:8, :]
    shape = rows.shape[1:]
    lane, row = lane_of(shape), row_of(shape)
    after = lax.rem(lax.axis_index("gx") + 1, count_x)
    for owner in range(count_x):
        number = jnp.zeros(shape, jnp.int32)
        for rank in range(CAP):
            number = jnp.where(lane == rank, id_ref[owner * CAP + rank], number)
        value = jnp.where(after == owner, rows[1], rows[0])
        ask[owner] = jnp.where(row == 18, number.astype(F32), value)


def columns_of(shape):
    lane = lane_of(shape)
    key = lax.rem(lane, 24)
    col = 32 * (key & 3) + (key >> 3) + jnp.where((key & 4) == 0, -2, 31)
    return lane, col & (LANES - 1)


def place_columns(z, d, start, count, value):
    group, part = divmod(d, 5)
    lane, col = columns_of((count, LANES))
    got = take_lanes(value, col)
    if part:
        inside = (lane >= 24 * part) & (lane < 24 * part + 24)
        got = jnp.where(inside, got, z[group, pl.ds(start, count), :])
    z[group, pl.ds(start, count), :] = got


def turn_columns(z, sets, to_high, to_low):
    to_high[...] = jnp.full(to_high.shape, 0.1, F32)
    to_low[...] = jnp.full(to_low.shape, 0.1, F32)
    for group in range(2):
        for t in range(z.shape[1] // LANES):
            lanes = pl.ds(t * LANES, LANES)
            turned = z[group, t * LANES : (t + 1) * LANES, :].T
            for part in range(5 - group):
                d = 5 * group + part
                for s in range(3):
                    sets[s, d, :, lanes] = turned[24 * part + 8 * s : 24 * part + 8 * s + 8]
                base = 24 * part
                to_high[2 * d : 2 * d + 1, lanes] = turned[base : base + 1]
                to_high[2 * d + 1 : 2 * d + 2, lanes] = turned[base + 8 : base + 9]
                to_low[2 * d : 2 * d + 1, lanes] = turned[base + 15 : base + 16]
                to_low[2 * d + 1 : 2 * d + 2, lanes] = turned[base + 23 : base + 24]


def pack_kernel(coarse, sets, to_high, to_low, buf, z, sems):
    width = coarse.shape[1]
    copies = [pltpu.make_async_copy(coarse.at[d], buf.at[d], sems.at[d]) for d in range(9)]
    for copy in copies:
        copy.start()
    rows = 512
    for d in range(9):
        copies[d].wait()

        def chunk(k, carry, d=d):
            start = pl.multiple_of(k * rows, rows)
            place_columns(z, d, start, rows, buf[d, pl.ds(start, rows), :])
            return carry

        lax.fori_loop(0, width // rows, chunk, 0)
    turn_columns(z, sets, to_high, to_low)


def neighbours(count_x):
    index = lax.axis_index("gx")
    return lax.rem(index + count_x - 1, count_x), lax.rem(index + 1, count_x)


def corner_kernel(count_x, asked, sets, to_high, to_low, ext, z):
    before, after = neighbours(count_x)
    ext[...] = jnp.full(ext.shape, 0.1, F32)
    z[...] = jnp.full(z.shape, 0.1, F32)
    for d in range(9):
        ext[0, d, 0:2, :] = asked[after, 2 * d : 2 * d + 2, :]
        ext[1, d, 6:8, :] = asked[before, 2 * d : 2 * d + 2, :]
    for d in range(9):
        place_columns(z, d, 0, 8, ext[0, d])
        place_columns(z, d, LANES - 8, 8, ext[1, d])
    turn_columns(z, sets, to_high, to_low)


def window(parts, j, off):
    lane = lane_of((8, LANES))
    before, value, after = parts
    shift = (WINDOW * j - off + 1) % LANES

    def move(part):
        return pltpu.roll(part, shift, 1) if shift else part

    value = move(value)
    if off == 0:
        value = jnp.where(lane == WINDOW * j, move(before), value)
    if off == LANES - COARSE_EDGE:
        value = jnp.where(lane == WINDOW * j + COARSE_EDGE + 1, move(after), value)
    return value


def join(parts):
    lane = lane_of((8, LANES))
    first, second, third = parts
    return jnp.where(lane < WINDOW, first, jnp.where(lane < 2 * WINDOW, second, third))


def ghost_kernel(
    count_x,
    count_y,
    coarse,
    asked,
    sets_main,
    low_main,
    high_main,
    sets_ext,
    low_ext,
    high_ext,
    message,
    inject_hbm,
    ids,
    numbers,
    first,
    last,
    turn,
    mt,
    old_t,
    post_t,
    new_t,
    g_t,
    pack_t,
    raw_r,
    post_r,
    new_r,
    g_r,
    far,
    pack_r,
    inject,
    sems,
):
    blocks_x = coarse.shape[1]
    width = blocks_x * COARSE_EDGE
    wide = width + LANES
    tiles = wide // LANES
    width_y = LANES
    blocks_y = width_y // COARSE_EDGE
    total_y = width_y * count_y
    base_y = lax.axis_index("gy") * width_y
    copy_first = pltpu.make_async_copy(coarse.at[:, :, pl.ds(0, 8), :], first, sems.at[0])
    copy_last = pltpu.make_async_copy(
        coarse.at[:, :, pl.ds(COARSE_EDGE - 8, 8), :], last, sems.at[1]
    )
    copy_first.start()
    copy_last.start()
    copy_ids = pltpu.make_async_copy(asked.at[:, pl.ds(16, 8), :], numbers, sems.at[2])
    copy_ids.start()
    index_before, index_after = neighbours(count_x)

    turn[...] = jnp.full(turn.shape, 0.1, F32)
    for d in range(9):
        at = (4 * d - 2) % LANES
        turn[4 * d : 4 * d + 2, 0:width] = high_main[2 * d : 2 * d + 2, :]
        turn[4 * d : 4 * d + 2, width:] = high_ext[2 * d : 2 * d + 2, :]
        turn[at : at + 2, 0:width] = low_main[2 * d : 2 * d + 2, :]
        turn[at : at + 2, width:] = low_ext[2 * d : 2 * d + 2, :]
    for t in range(tiles):
        mt[t * LANES : (t + 1) * LANES, :] = turn[:, t * LANES : (t + 1) * LANES].T
    tile = (8, LANES)
    row8 = row_of(tile)

    def collide_tile(sets, from_low, from_high, at, lanes):
        for s in range(3):
            p = []
            for d in range(9):
                value = sets[s, d, :, at]
                if s < 2:
                    value = jnp.where(row8 == 0, from_low[2 * d + s : 2 * d + s + 1, at], value)
                if s > 0:
                    value = jnp.where(row8 == 7, from_high[2 * d + s - 1 : 2 * d + s, at], value)
                if s == 1:
                    old_t[d, :, lanes] = value
                p.append(value)
            out = relax(p, COARSE)
            for d in range(9):
                post_t[s, d, :, lanes] = out[d]

    def collide_t(t, carry):
        lanes = pl.ds(pl.multiple_of(t * LANES, LANES), LANES)
        collide_tile(sets_main, low_main, high_main, lanes, lanes)
        return carry

    lax.fori_loop(0, tiles - 1, collide_t, 0)
    collide_tile(sets_ext, low_ext, high_ext, pl.ds(0, LANES), pl.ds(width, LANES))
    turn[...] = jnp.zeros(turn.shape, F32)
    row_t = row_of((8, wide))
    coord_t = base_y + 32 * (row_t & 3) + jnp.where(row_t < 4, -1, 32)
    for d in range(9):
        source = post_t[{1: 0, 0: 1, -1: 2}[along_y[d]], d]
        if along_x[d]:
            source = pltpu.roll(source, along_x[d] % wide, 1)
        back = coord_t - along_y[d]
        beyond = (back < 0) | (back >= total_y)
        new_t[d] = jnp.where(beyond, post_t[1, opposite[d]], source)
    for j in range(3):
        for side, (d, row) in enumerate(((LEFT[j], 0), (RIGHT[j], 7))):
            source = post_t[1, d]
            if along_x[d]:
                source = pltpu.roll(source, along_x[d] % wide, 1)
            turn[3 * side + j : 3 * side + j + 1, :] = source[row : row + 1, :]
    for t in range(width // LANES):
        inject[t * LANES : (t + 1) * LANES, :] = turn[:, t * LANES : (t + 1) * LANES].T
    copy_inject = pltpu.make_async_copy(inject, inject_hbm, sems.at[3])
    copy_inject.start()

    def ghosts_t(t, carry):
        lanes = pl.ds(pl.multiple_of(t * LANES, LANES), LANES)
        old = [old_t[d, :, lanes] for d in range(9)]
        mean = [0.5 * (old[d] + new_t[d, :, lanes]) for d in range(9)]
        for sub, p in enumerate((old, mean)):
            out = relax(p, GHOST, LEFT + RIGHT)
            for j in range(3):
                g_t[sub, j, :, lanes] = jnp.where(row8 < 4, out[LEFT[j]], out[RIGHT[j]])
        return carry

    lax.fori_loop(0, tiles, ghosts_t, 0)
    for sub in range(2):
        for bx in range(blocks_x):
            t, off = divmod(COARSE_EDGE * bx, LANES)
            near = [(t + step) % tiles for step in (-1, 0, 1)]
            got = []
            for j in range(3):
                parts = [g_t[sub, j, :, LANES * k : LANES * (k + 1)] for k in near]
                got.append(window(parts, j, off))
            pack_t[sub, bx] = join(got)

    plane = (blocks_x, LANES)
    rows_b = row_of(plane)

    def lower(value, row):
        return jnp.where(rows_b == 0, row, pltpu.roll(value, 1, 0))

    def upper(value, row):
        return jnp.where(rows_b == blocks_x - 1, row, pltpu.roll(value, blocks_x - 1, 0))

    def every(ref, start, step):
        return ref[pl.ds(start, blocks_x, stride=step), :]

    side_rows = [every(mt, c, COARSE_EDGE) for c in (0, 1, COARSE_EDGE - 2, COARSE_EDGE - 1)]
    m0, m1, m30, m31 = side_rows
    extra = (
        lower(m30, mt[wide - 2 : wide - 1, :]),
        lower(m31, mt[wide - 1 : wide, :]),
        m0,
        m31,
        upper(m0, mt[width : width + 1, :]),
        upper(m1, mt[width + 1 : width + 2, :]),
    )
    copy_first.wait()
    copy_last.wait()
    first2 = first.reshape(9 * blocks_x * 8, LANES)
    last2 = last.reshape(9 * blocks_x * 8, LANES)
    for k in range(6):
        far[k] = extra[k]

    def raw_rows(d, carry):
        at = d * (blocks_x * 8)
        a0, a1 = every(first2, at, 8), every(first2, at + 1, 8)
        b30, b31 = every(last2, at + 6, 8), every(last2, at + 7, 8)
        main = (
            lower(b30, asked[index_before, pl.ds(2 * d, 1), :]),
            lower(b31, asked[index_before, pl.ds(2 * d + 1, 1), :]),
            a0,
            b31,
            upper(a0, asked[index_after, pl.ds(2 * d, 1), :]),
            upper(a1, asked[index_after, pl.ds(2 * d + 1, 1), :]),
        )
        for k in range(6):
            raw_r[k, d, :, 0:LANES] = main[k]
            raw_r[k, d, :, LANES:] = pltpu.roll(far[k], lax.rem(LANES - 4 * d, LANES), 1)
        return carry

    lax.fori_loop(0, 9, raw_rows, 0)

    def collide_r(k, carry):
        rows = pl.ds(pl.multiple_of(k * 8, 8), 8)
        for s in range(6):
            for half in range(2):
                lanes = pl.ds(half * LANES, LANES)
                out = relax([raw_r[s, d, rows, lanes] for d in range(9)], COARSE)
                for d in range(9):
                    post_r[s, d, rows, lanes] = out[d]
        return carry

    lax.fori_loop(0, blocks_x // 8, collide_r, 0)
    double = (8, 2 * LANES)
    lane_r = lane_of(double)
    coord_r = base_y + jnp.where(lane_r < LANES + 2, lane_r, lane_r - 2 * LANES)

    def ghosts_r(k, carry):
        rows = pl.ds(pl.multiple_of(k * 8, 8), 8)
        for side in range(2):
            for d in range(9):
                source = post_r[3 * side + {1: 0, 0: 1, -1: 2}[along_x[d]], d, rows, :]
                if along_y[d]:
                    source = pltpu.roll(source, along_y[d] % (2 * LANES), 1)
                back = coord_r - along_y[d]
                beyond = (back < 0) | (back >= total_y)
                new_r[d] = jnp.where(beyond, post_r[3 * side + 1, opposite[d], rows, :], source)
            which = (UP, DOWN)[side]
            for half in range(2):
                lanes = pl.ds(half * LANES, LANES)
                old = [raw_r[3 * side + 1, d, rows, lanes] for d in range(9)]
                mean = [0.5 * (old[d] + new_r[d, :, lanes]) for d in range(9)]
                for sub, p in enumerate((old, mean)):
                    out = relax(p, GHOST, which)
                    for j in range(3):
                        g_r[side, j, sub, rows, lanes] = out[which[j]]
        return carry

    lax.fori_loop(0, blocks_x // 8, ghosts_r, 0)

    def windows_r(k, carry):
        rows = pl.ds(pl.multiple_of(k * 8, 8), 8)
        for side in range(2):
            for sub in range(2):
                for by in range(blocks_y):
                    got = []
                    for j in range(3):
                        one = g_r[side, j, sub, rows, 0:LANES]
                        two = g_r[side, j, sub, rows, LANES:]
                        got.append(window((two, one, two), j, COARSE_EDGE * by))
                    pack_r[side, sub, by, rows, :] = join(got)
        return carry

    lax.fori_loop(0, blocks_x // 8, windows_r, 0)

    copy_ids.wait()
    for q in range(message.shape[0]):
        ids[q] = numbers[q // CAP, 2, q % CAP].astype(jnp.int32)

    def pick(q, carry):
        block = jnp.maximum(ids[q], 0)
        bx = lax.div(block, blocks_y)
        by = block - bx * blocks_y
        for sub in range(2):
            for side in range(2):
                row = 4 * sub + side
                message[q, row : row + 1, :] = pack_r[side, sub, by, pl.ds(bx, 1), :]
                row = 4 * sub + 2 + side
                message[q, row : row + 1, :] = pack_t[sub, bx, pl.ds(4 * side + by, 1), :]
        return carry

    lax.fori_loop(0, message.shape[0], pick, 0)
    copy_inject.wait()


def start_kernel(slot, fine, post, sem):
    places = post.shape[1]
    copies = []
    for q in range(places):
        source = fine.at[:, pl.ds(jnp.maximum(slot[q], 0), 1), :]
        copy = pltpu.make_async_copy(source, post.at[:, pl.ds(q, 1), :], sem.at[q])
        copy.start()
        copies.append(copy)
    for copy in copies:
        copy.wait()

    def body(k, carry):
        lanes = pl.ds(pl.multiple_of(k * LANES, LANES), LANES)
        for h in range(places // 8):
            rows = pl.ds(8 * h, 8)
            out = relax([post[d, rows, lanes] for d in range(9)], FINE)
            for d in range(9):
                post[d, rows, lanes] = out[d]
        return carry

    lax.fori_loop(0, post.shape[2] // LANES, body, 0, unroll=2)


def fine_kernel(slot, post, ghosts, fine, back, result, post_two, line, mean, swapped, sem):
    places = post.shape[1]
    tiles = post.shape[2] // LANES
    tile = (8, LANES)
    lane, row = lane_of(tile), row_of(tile)
    low_half = lane < 64
    at_low = (lane & 63) == 0
    at_high = (lane & 63) == 63
    ghosts2 = ghosts.reshape(places * 8, LANES)
    over = [WINDOW * j + 1 + (((lane & 63) - c) >> 1) for j, c in enumerate(ORDER)]
    even = (lane & 1) == 0
    turn_back = jnp.where(even, lane, (lane - 63) & (LANES - 1))
    cell = (turn_back & 63) + (turn_back >> 6)
    along = [(WINDOW * j + 1 + ((cell - c) >> 1)) & (LANES - 1) for j, c in enumerate(ORDER)]
    squeeze = 64 * ((lane >> 5) & 1) + 2 * (lane & 31) + (lane >> 6)

    def copy(q):
        target = fine.at[:, pl.ds(jnp.maximum(slot[q], 0), 1), :]
        return pltpu.make_async_copy(result.at[:, pl.ds(q, 1), :], target, sem.at[q])

    def half(h, carry):
        rows = pl.ds(pl.multiple_of(8 * h, 8), 8)
        wall = jnp.zeros(tile, jnp.int32)
        for r in range(8):
            wall = jnp.where(row == r, slot[places + 8 * h + r], wall)
        wall_low = at_low & ((wall & 1) != 0)
        wall_high = at_high & ((wall & 2) != 0)

        def substep(sub, source, emit):
            border = [
                ghosts2[pl.ds(h * 64 + 4 * sub + side, 8, stride=8), :] for side in range(4)
            ]
            up = [take_lanes(border[0], over[j]) for j in range(3)]
            down = [take_lanes(border[1], over[j]) for j in range(3)]
            beside = [
                jnp.where(even, take_lanes(border[2], along[j]), take_lanes(border[3], along[j]))
                for j in range(3)
            ]

            def load(d, k):
                return source[d, rows, k * LANES : (k + 1) * LANES]

            def crossed(d, k):
                if k < 0:
                    return up[UP.index(d)]
                if k == tiles:
                    return down[DOWN.index(d)]
                return pltpu.roll(load(d, k), (64 + along_y[d]) % LANES, 1)

            before = {d: crossed(d, -1) for d in UP}
            now = {d: crossed(d, 0) for d in DOWN}
            for k in range(tiles):
                ghosts_k = [
                    pltpu.roll(value, (-2 * k) % LANES, 1) if k else value for value in beside
                ]
                out = []
                for d in range(9):
                    if along_x[d] > 0:
                        turned = crossed(d, k)
                        value = jnp.where(low_half, before[d], turned)
                        before[d] = turned
                    elif along_x[d] < 0:
                        turned = crossed(d, k + 1)
                        value = jnp.where(low_half, now[d], turned)
                        now[d] = turned
                    else:
                        value = load(d, k)
                        if along_y[d]:
                            value = pltpu.roll(value, along_y[d] % LANES, 1)
                    if along_y[d] > 0:
                        value = jnp.where(at_low, ghosts_k[LEFT.index(d)], value)
                        value = jnp.where(wall_low, load(opposite[d], k), value)
                    elif along_y[d] < 0:
                        value = jnp.where(at_high, ghosts_k[RIGHT.index(d)], value)
                        value = jnp.where(wall_high, load(opposite[d], k), value)
                    out.append(value)
                emit(k, out)

        def emit_first(k, p):
            out = relax(p, FINE)
            for d in range(9):
                post_two[d, :, k * LANES : (k + 1) * LANES] = out[d]

        def emit_second(k, p):
            for d in range(9):
                result[d, rows, k * LANES : (k + 1) * LANES] = p[d]

        post_rows = post
        substep(0, post_rows, emit_first)
        substep(1, _Rows(post_two), emit_second)
        for r in range(8):

            @pl.when(slot[8 * h + r] >= 0)
            def _(r=r):
                copy(8 * h + r).start()

        def tile_of(ref, d, k):
            return ref[d, rows, pl.ds(pl.multiple_of(k * LANES, LANES), LANES)]

        def pair_up(step, carry):
            for u in range(4):
                i = 4 * step + u
                for d in range(9):
                    pairs = []
                    for m in range(2):
                        one = tile_of(result, d, i + 16 * m)
                        two = tile_of(result, d, i + 16 * m + 8)
                        other = pltpu.roll(jnp.where(low_half, two, one), 64, 1)
                        pairs.append(jnp.where(low_half, one, two) + other)
                    mean[d, i] = jnp.where(even, pairs[0], pairs[1])
                    swapped[d, i] = jnp.where(even, pairs[1], pairs[0])
            return carry

        def merge(step, carry):
            for u in range(4):
                i = 4 * step + u
                total = []
                for d in range(9):
                    moved = swapped[d, i]
                    moved = jnp.where(even, pltpu.roll(moved, 127, 1), pltpu.roll(moved, 1, 1))
                    total.append(0.25 * (mean[d, i] + moved))
                out = relax(total, COALESCE)
                for d in range(9):
                    mean[d, i] = out[d]
            return carry

        def compress(step, carry):
            for u in range(4):
                i = 4 * step + u
                for d in range(9):
                    at = pl.ds(pl.multiple_of(i * 8, 8), 8)
                    line[d, at, :] = take_lanes(mean[d, i], squeeze)
            return carry

        lax.fori_loop(0, 2, pair_up, 0)
        lax.fori_loop(0, 2, merge, 0)
        lax.fori_loop(0, 2, compress, 0)
        for d in range(9):
            flat = line.at[d]
            for q in range(8):
                back[8 * h + q, d * 8 : d * 8 + 8, :] = flat[pl.ds(q, 8, stride=8), :]
        return carry

    lax.fori_loop(0, places // 8, half, 0)
    for q in range(places):

        @pl.when(slot[q] >= 0)
        def _(q=q):
            copy(q).wait()


class _Rows:
    def __init__(self, ref):
        self.ref = ref

    def __getitem__(self, key):
        d, _, lanes = key
        return self.ref[d, :, lanes]


def coarse_kernel(
    count_x, count_y, coarse, asked, inject_hbm, after, ids, base, strips, home, inject, new, post, load, save, cut
):
    width = coarse.shape[1]
    places = ids.shape[0]
    blocks_y = coarse.shape[2] // COARSE_EDGE
    tile = (8, LANES)
    lane = lane_of(tile)
    parts = 4
    size = width // parts
    copies = [
        pltpu.make_async_copy(
            coarse.at[:, pl.ds(k * size, size), :],
            post.at[:, pl.ds(8 + k * size, size), :],
            load.at[k],
        )
        for k in range(parts)
    ]
    for copy in copies:
        copy.start()
    copy_inject = pltpu.make_async_copy(inject_hbm, inject, load.at[parts])
    copy_inject.start()
    before, following = neighbours(count_x)
    out = relax([asked[before, 2 * d + 1 : 2 * d + 2, :] for d in range(9)], COARSE)
    for d in range(9):
        post[d, 7:8, :] = out[d]
    out = relax([asked[following, 2 * d : 2 * d + 1, :] for d in range(9)], COARSE)
    for d in range(9):
        post[d, width + 8 : width + 9, :] = out[d]

    def collide(k, carry):
        rows = pl.ds(pl.multiple_of(8 + 8 * k, 8), 8)
        out = relax([post[d, rows, :] for d in range(9)], COARSE)
        for d in range(9):
            post[d, rows, :] = out[d]
        return carry

    index_y = lax.axis_index("gy")
    wall_low = (lane == 0) & (index_y == 0)
    wall_high = (lane == LANES - 1) & (index_y == count_y - 1)

    def stream(k, carry):
        start = pl.multiple_of(8 * k, 8)
        edge = inject[pl.ds(start, 8), :]
        for d in range(9):
            value = post[d, pl.ds(start + (8 - along_x[d]), 8), :]
            if along_y[d]:
                value = pltpu.roll(value, along_y[d] % LANES, 1)
                same = post[opposite[d], pl.ds(start + 8, 8), :]
                if along_y[d] > 0:
                    j = LEFT.index(d)
                    value = jnp.where(lane == 0, pltpu.roll(edge, (-j) % LANES, 1), value)
                    value = jnp.where(wall_low, same, value)
                else:
                    j = RIGHT.index(d)
                    moved = pltpu.roll(edge, LANES - 4 - j, 1)
                    value = jnp.where(lane == LANES - 1, moved, value)
                    value = jnp.where(wall_high, same, value)
            new[d, pl.ds(start, 8), :] = value
        return carry

    copy_inject.wait()
    copies[0].wait()
    lax.fori_loop(0, size // 8, collide, 0, unroll=4)
    stores = []
    for k in range(parts):
        if k + 1 < parts:
            copies[k + 1].wait()
            lax.fori_loop((k + 1) * size // 8, (k + 2) * size // 8, collide, 0, unroll=4)
        lax.fori_loop(k * size // 8, (k + 1) * size // 8, stream, 0, unroll=4)
        rows = pl.ds(k * size, size)
        store = pltpu.make_async_copy(new.at[:, rows, :], base.at[:, rows, :], save.at[k])
        store.start()
        stores.append(store)

    def column(q):
        return lax.div(jnp.maximum(ids[q], 0), blocks_y)

    def strip(q):
        rows = pl.ds(pl.multiple_of(COARSE_EDGE * column(q), COARSE_EDGE), COARSE_EDGE)
        return pltpu.make_async_copy(
            new.at[:, rows, :], strips.at[:, pl.ds(COARSE_EDGE * q, COARSE_EDGE), :], cut.at[q]
        )

    for q in range(places):

        @pl.when(ids[q] >= 0)
        def _(q=q):
            strip(q).start()

    for q in range(places):
        first, last = jnp.int32(q), jnp.int32(1)
        for other in reversed(range(places)):
            if other != q:
                same = (ids[q] >= 0) & (ids[other] >= 0) & (column(q) == column(other))
                if other < q:
                    first = jnp.where(same, other, first)
                else:
                    last = jnp.where(same, 0, last)
        home[q] = first
        home[places + q] = last
    for store in stores:
        store.wait()
    for q in range(places):

        @pl.when(ids[q] >= 0)
        def _(q=q):
            strip(q).wait()


def patch_kernel(blocks_y, ids, home, base, strips_in, back, strips, out, save):
    lane = lane_of((8, LANES))
    places = ids.shape[0]

    def store(q):
        bx = lax.div(jnp.maximum(ids[q], 0), blocks_y)
        rows = pl.ds(pl.multiple_of(COARSE_EDGE * bx, COARSE_EDGE), COARSE_EDGE)
        own = pl.ds(pl.multiple_of(COARSE_EDGE * home[q], COARSE_EDGE), COARSE_EDGE)
        return pltpu.make_async_copy(strips.at[:, own, :], out.at[:, rows, :], save.at[q])

    def patch(q, carry):
        @pl.when(ids[q] >= 0)
        def _():
            by = lax.rem(ids[q], blocks_y)
            inside = (lane >> 5) == by
            start = pl.multiple_of(COARSE_EDGE * home[q], COARSE_EDGE)
            for group in (range(5), range(5, 9)):
                merged = []
                for d in group:
                    value = back[q, d * 8 : d * 8 + 8, :]
                    for j in range(4):
                        moved = pltpu.roll(value, lax.rem(by + 4 - j, 4) * 32, 1)
                        merged.append((d, pl.ds(start + 8 * j, 8), moved))
                merged = [
                    (d, rows, jnp.where(inside, moved, strips[d, rows, :]))
                    for d, rows, moved in merged
                ]
                for d, rows, value in merged:
                    strips[d, rows, :] = value

        @pl.when((ids[q] >= 0) & (home[places + q] == 1))
        def _():
            store(q).start()

        return carry

    lax.fori_loop(0, places, patch, 0)
    for q in range(places):

        @pl.when((ids[q] >= 0) & (home[places + q] == 1))
        def _(q=q):
            store(q).wait()


def in_hbm(value):
    return pltpu.with_memory_space_constraint(value, pltpu.HBM)


def in_vmem(value):
    return pltpu.with_memory_space_constraint(value, pltpu.VMEM)


def local(coarse_pop, fine_pop, fine_block):
    width_x, width_y = coarse_pop.shape[1:]
    blocks_x = width_x // COARSE_EDGE
    blocks_y = width_y // COARSE_EDGE
    count_x = lax.axis_size("gx")
    count_y = lax.axis_size("gy")
    columns = blocks_y * count_y
    places = count_x * CAP
    slots = fine_block.shape[0]
    cells = FINE_EDGE * FINE_EDGE
    wide = width_x + LANES
    smem = pl.BlockSpec(memory_space=pltpu.SMEM)
    vmem = pl.BlockSpec(memory_space=pltpu.VMEM)
    hbm = pl.BlockSpec(memory_space=pltpu.HBM)
    sds = jax.ShapeDtypeStruct

    def held(*shape):
        return pltpu.VMEM(shape, F32)

    ask, slot = pl.pallas_call(
        functools.partial(ask_kernel, columns, blocks_x, blocks_y, count_x),
        out_shape=(held(count_x, 24, LANES), sds((2 * places,), jnp.int32)),
        in_specs=[hbm, hbm],
        out_specs=(vmem, smem),
        scratch_shapes=[
            pltpu.SMEM((slots,), jnp.int32),
            pltpu.SMEM((places,), jnp.int32),
            pltpu.SMEM((count_x,), jnp.int32),
            held(2, 9, 8, LANES),
            held(2, 24, LANES),
            pltpu.SemaphoreType.DMA((3,)),
        ],
        name="ask",
        compiler_params=GRANT,
    )(in_hbm(fine_block), in_hbm(coarse_pop))
    asked = in_vmem(lax.all_to_all(ask, "gx", split_axis=0, concat_axis=0, tiled=True))
    forward_y = [(i, (i + 1) % count_y) for i in range(count_y)]
    backward_y = [(target, source) for source, target in forward_y]

    def columns_round(packed):
        sets, to_high, to_low = packed
        from_low = lax.ppermute(to_high, "gy", forward_y)
        from_high = lax.ppermute(to_low, "gy", backward_y)
        return [in_vmem(value) for value in (sets, from_low, from_high)]

    main = columns_round(
        pl.pallas_call(
            pack_kernel,
            out_shape=(held(3, 9, 8, width_x), held(24, width_x), held(24, width_x)),
            in_specs=[hbm],
            out_specs=(vmem, vmem, vmem),
            scratch_shapes=[
                held(9, width_x, LANES),
                held(2, width_x, LANES),
                pltpu.SemaphoreType.DMA((9,)),
            ],
            name="pack",
        compiler_params=GRANT,
        )(in_hbm(coarse_pop))
    )
    corner = columns_round(
        pl.pallas_call(
            functools.partial(corner_kernel, count_x),
            out_shape=(held(3, 9, 8, LANES), held(24, LANES), held(24, LANES)),
            in_specs=[vmem],
            out_specs=(vmem, vmem, vmem),
            scratch_shapes=[held(2, 9, 8, LANES), held(2, LANES, LANES)],
            name="corner",
        compiler_params=GRANT,
        )(asked)
    )
    fine_turned = jnp.transpose(fine_pop, (1, 0, 2))
    post = pl.pallas_call(
        start_kernel,
        out_shape=held(9, places, cells),
        in_specs=[smem, hbm],
        out_specs=vmem,
        scratch_shapes=[pltpu.SemaphoreType.DMA((places,))],
        name="start",
        compiler_params=GRANT,
    )(slot, in_hbm(fine_turned))
    message, inject, wanted = pl.pallas_call(
        functools.partial(ghost_kernel, count_x, count_y),
        out_shape=(
            held(places, 8, LANES),
            pltpu.HBM((width_x, LANES), F32),
            sds((places,), jnp.int32),
        ),
        in_specs=[hbm] + [vmem] * 7,
        out_specs=(vmem, hbm, smem),
        scratch_shapes=[
            pltpu.SMEM((count_x, 8, LANES), F32),
            held(9, blocks_x, 8, LANES),
            held(9, blocks_x, 8, LANES),
            held(LANES, wide),
            held(wide, LANES),
            held(9, 8, wide),
            held(3, 9, 8, wide),
            held(9, 8, wide),
            held(2, 3, 8, wide),
            held(2, blocks_x, 8, LANES),
            held(6, 9, blocks_x, 2 * LANES),
            held(6, 9, blocks_x, 2 * LANES),
            held(9, 8, 2 * LANES),
            held(2, 3, 2, blocks_x, 2 * LANES),
            held(6, blocks_x, LANES),
            held(2, 2, blocks_y, blocks_x, LANES),
            held(width_x, LANES),
            pltpu.SemaphoreType.DMA((4,)),
        ],
        name="ghost",
        compiler_params=GRANT,
    )(in_hbm(coarse_pop.reshape(9, blocks_x, COARSE_EDGE, width_y)), asked, *main, *corner)
    ghosts = in_vmem(lax.all_to_all(message, "gx", split_axis=0, concat_axis=0, tiled=True))
    fine_out, back = pl.pallas_call(
        fine_kernel,
        out_shape=(pltpu.HBM((9, slots, cells), F32), held(places, 72, LANES)),
        in_specs=[smem, vmem, vmem],
        out_specs=(hbm, vmem),
        scratch_shapes=[
            held(9, places, cells),
            held(9, 8, cells),
            held(9, 64, LANES),
            held(9, 8, 8, LANES),
            held(9, 8, 8, LANES),
            pltpu.SemaphoreType.DMA((places,)),
        ],
        name="fine",
        compiler_params=GRANT,
    )(slot, in_vmem(post), ghosts)
    returned = in_vmem(lax.all_to_all(back, "gx", split_axis=0, concat_axis=0, tiled=True))
    base, strips, home = pl.pallas_call(
        functools.partial(coarse_kernel, count_x, count_y),
        out_shape=(
            pltpu.HBM((9, width_x, width_y), F32),
            held(9, COARSE_EDGE * places, width_y),
            sds((2 * places,), jnp.int32),
        ),
        in_specs=[hbm, vmem, hbm, vmem, smem],
        out_specs=(hbm, vmem, smem),
        scratch_shapes=[
            held(width_x, LANES),
            held(9, width_x, LANES),
            held(9, width_x + 16, LANES),
            pltpu.SemaphoreType.DMA((5,)),
            pltpu.SemaphoreType.DMA((4,)),
            pltpu.SemaphoreType.DMA((places,)),
        ],
        name="coarse",
        compiler_params=GRANT,
    )(in_hbm(coarse_pop), asked, in_hbm(inject), in_vmem(back), wanted)
    _, coarse_out = pl.pallas_call(
        functools.partial(patch_kernel, blocks_y),
        out_shape=(
            held(9, COARSE_EDGE * places, width_y),
            pltpu.HBM((9, width_x, width_y), F32),
        ),
        in_specs=[smem, smem, hbm, vmem, vmem],
        out_specs=(vmem, hbm),
        scratch_shapes=[pltpu.SemaphoreType.DMA((places,))],
        input_output_aliases={2: 1, 3: 0},
        name="patch",
        compiler_params=GRANT,
    )(wanted, home, in_hbm(base), in_vmem(strips), returned)
    return (coarse_out, jnp.transpose(fine_out, (1, 0, 2)))


def solution(mesh):
    return jax.shard_map(
        local,
        mesh=mesh,
        in_specs=(P(None, "gx", "gy"), P(("gx", "gy"), None, None), P(("gx", "gy"))),
        out_specs=(P(None, "gx", "gy"), P(("gx", "gy"), None, None)),
        check_vma=False,
    )
```

time: 104 us -> 66.5 us (0.64)
  Pallas kernels: 63.5 us -> 34.2 us
  blocking collectives: 8.85 us -> 0 us
  local copies, waits for them, and re-layouts: 5.43 us -> 0 us
  starting transfers between devices: 15.3 us -> 19.2 us
  waiting for transfers between devices: 8.62 us -> 12 us
    pallas_call x8, Pallas kernels: 63.5 us -> 34.2 us  [the longest x1 10.9 us: local(): pl.pallas_call(functools.partial(coarse_kernel, count_x, count_y), out_sh...]
    all_to_all x1 -> x0, blocking collectives: 8.85 us -> none  [local(): wanted = lax.all_to_all(ids, 'gx', split_axis=0, concat_axis=0, tiled=True)]
    all_to_all x0 -> x1, starting transfers between devices: none -> 7.29 us  [local(): lax.all_to_all(ask, 'gx', split_axis=0, concat_axis=0, tiled=True)]
    all_to_all x1, waiting for transfers between devices: 0.39 us -> 5.55 us  [local(): lax.all_to_all(back, 'gx', split_axis=0, concat_axis=0, tiled=True)]
    ppermute x4, waiting for transfers between devices: 6.36 us -> 1.4 us  [the longest x2 1.37 us: columns_round(): from_low = lax.ppermute(to_high, 'gy', forward_y)]
    ppermute x4, starting transfers between devices: 7.84 us -> 3.58 us  [the longest x2 3.47 us: columns_round(): from_high = lax.ppermute(to_low, 'gy', backward_y)]
    unnamed x12 -> x0, local copies, waits for them, and re-layouts: 2.72 us -> none
    all_to_all x3 -> x0, local copies, waits for them, and re-layouts: 1.91 us -> none  [local(): wanted = lax.all_to_all(ids, 'gx', split_axis=0, concat_axis=0, tiled=True)]
  transfers between devices with their start and end apart: 6 -> 7, of which waited for: 4 -> 4; matrix products, arithmetic and copies ran while one was open for 1% -> 0% of each run, Pallas kernels for 20% -> 28%
where the time goes in v2:
time: 66.5 us; the launch traced here: 66 us
  Pallas kernels  34.2 us (51%)
  starting transfers between devices  19.2 us (29%)
  waiting for transfers between devices  12 us (18%)
  between operations  0.71 us (1%)
    pallas_call x1, Pallas kernels, local(): pl.pallas_call(functools.partial(coarse_kernel, count_x, count_y), out_sh...  10.9 us
    all_to_all x1, starting transfers between devices, local(): lax.all_to_all(ask, 'gx', split_axis=0, concat_axis=0, tiled=True)  7.29 us
    pallas_call x1, Pallas kernels, local(): pl.pallas_call(fine_kernel, out_shape=(pltpu.HBM((9, slots, cells), F32),...  5.57 us
    all_to_all x1, waiting for transfers between devices, local(): lax.all_to_all(back, 'gx', split_axis=0, concat_axis=0, tiled=True)  5.55 us
    pallas_call x1, Pallas kernels, local(): pl.pallas_call(functools.partial(ghost_kernel, count_x, count_y), out_sha...  5.18 us
    all_to_all x1, starting transfers between devices, local(): lax.all_to_all(message, 'gx', split_axis=0, concat_axis=0, tiled=True)  4.73 us
    pallas_call x1, Pallas kernels, local(): pl.pallas_call(pack_kernel, out_shape=(held(3, 9, 8, width_x), held(24, w...  3.93 us
    all_to_all x1, waiting for transfers between devices, local(): lax.all_to_all(message, 'gx', split_axis=0, concat_axis=0, tiled=True)  3.64 us
  transfers between devices with their start and end apart: 7, of which 4 were waited for; matrix products, arithmetic and copies ran while one was open for 0% of the time, Pallas kernels for 28%

profile of v2, /device:TPU:0, one launch (start us, length us, event | category | flops | bytes accessed | tf_op | source)
XLA Modules:
  0.0 66.0 jit_solution(15575161312087154978)
XLA Ops:
  0.6 1.6 %ask.1 = (f32[8,24,128]{2,1,0:T(8,128)}, s32[32]{0:T(128)S(1)}) custom-call(s32[16]{0:T(128)} %block_hbm.1, f32[9,1024,128]{2,1,0:T(8,128)} %coarse.7), custom_call_target="tpu_custom_call" | custom-call | tf_op jit(solution)/shard_map/ask/pallas_call | solution.py:851
  2.2 7.3 %all-to-all-start = ((f32[8,24,128]{2,1,0:T(8,128)}), f32[8,24,128]{2,1,0:T(8,128)S(1)}, u32[]{:S(2)}, u32[]{:S(2)}) async-start(f32[8,24,128]{2,1,0:T(8,128)} %get-tuple-element.19), calls=%async_computation | async-start | bytes 196608 | tf_op jit(solution)/shard_map/all_to_all | solution.py:867
  9.5 3.9 %pack.1 = (f32[3,9,8,1024]{3,2,1,0:T(8,128)S(1)}, f32[24,1024]{1,0:T(8,128)S(1)}, f32[24,1024]{1,0:T(8,128)S(1)}) custom-call(f32[9,1024,128]{2,1,0:T(8,128)} %coarse.7), custom_call_target="tpu_custom_call" | custom-call | tf_op jit(solution)/shard_map/pack/pallas_call | solution.py:878
  13.4 0.1 collective-permute-start
  13.5 1.7 %collective-permute-start.1 = (f32[24,1024]{1,0:T(8,128)S(1)}, f32[24,1024]{1,0:T(8,128)S(1)}, u32[]{:S(2)}, u32[]{:S(2)}) collective-permute-start(f32[24,1024]{1,0:T(8,128)S(1)} %get-tuple-element.22), channel_id=1, source_target_pairs={{1,0},{2,1},{3,2},{0,3},{5,4},{6,5},{7,6},{4,7},{9,8},{10,9},{11,1... | collective-permute-start | bytes 294920 | tf_op jit(solution)/shard_map/ppermute | solution.py:874
  15.2 1.4 %all-to-all-done.asked = f32[8,24,128]{2,1,0:T(8,128)S(1)} async-done(((f32[8,24,128]{2,1,0:T(8,128)}), f32[8,24,128]{2,1,0:T(8,128)S(1)}, u32[]{:S(2)}, u32[]{:S(2)}) %all-to-all-start) | async-done | bytes 98336 | tf_op jit(solution)/shard_map/all_to_all | solution.py:867
  16.6 0.2 corner.1
  16.8 0.1 collective-permute-start.2
  16.9 1.7 %collective-permute-start.3 = (f32[24,128]{1,0:T(8,128)S(1)}, f32[24,128]{1,0:T(8,128)S(1)}, u32[]{:S(2)}, u32[]{:S(2)}) collective-permute-start(f32[24,128]{1,0:T(8,128)S(1)} %get-tuple-element.25), channel_id=1, source_target_pairs={{1,0},{2,1},{3,2},{0,3},{5,4},{6,5},{7,6},{4,7},{9,8},{10,9},{11,1... | collective-permute-start | bytes 36872 | tf_op jit(solution)/shard_map/ppermute | solution.py:874
  18.6 0.0 collective-permute-done.low_main
  18.6 0.0 collective-permute-done.1.high_main
  18.6 1.4 %collective-permute-done.2.low_ext = f32[24,128]{1,0:T(8,128)S(1)} collective-permute-done((f32[24,128]{1,0:T(8,128)S(1)}, f32[24,128]{1,0:T(8,128)S(1)}, u32[]{:S(2)}, u32[]{:S(2)}) %collective-permute-start.2) | collective-permute-done | bytes 12320 | tf_op jit(solution)/shard_map/ppermute | solution.py:873
  20.0 0.0 collective-permute-done.3.high_ext
  20.0 5.2 %ghost.1 = (f32[16,8,128]{2,1,0:T(8,128)}, f32[1024,128]{1,0:T(8,128)}, s32[16]{0:T(128)S(1)}) custom-call(f32[9,32,32,128]{3,2,1,0:T(8,128)} %bitcast.3, f32[8,24,128]{2,1,0:T(8,128)S(1)} %all-to-all-done.asked, f32[3,9,8,1024]{3,2,1,0:T(8,128)S(1)} %get-tuple-element.20.sets_main, f32[24,1024]{1,0:T(8,128)S(1)} %collective-permute-done.low_main, ...), custom_call_target="tpu_custom_call" | custom-call | tf_op jit(solution)/shard_map/ghost/pallas_call | solution.py:913
  25.2 4.7 %all-to-all-start.1 = ((f32[16,8,128]{2,1,0:T(8,128)}), f32[16,8,128]{2,1,0:T(8,128)S(1)}, u32[]{:S(2)}, u32[]{:S(2)}) async-start(f32[16,8,128]{2,1,0:T(8,128)} %get-tuple-element.29), calls=%async_computation.1 | async-start | bytes 131072 | tf_op jit(solution)/shard_map/all_to_all | solution.py:945
  29.9 3.4 %start.1.post = f32[9,16,4096]{2,1,0:T(8,128)S(1)} custom-call(s32[32]{0:T(128)S(1)} %get-tuple-element.28.slot, f32[9,16,4096]{2,1,0:T(8,128)} %bitcast.4), custom_call_target="tpu_custom_call" | custom-call | tf_op jit(solution)/shard_map/start/pallas_call | solution.py:904
  33.4 3.6 %all-to-all-done.1.ghosts = f32[16,8,128]{2,1,0:T(8,128)S(1)} async-done(((f32[16,8,128]{2,1,0:T(8,128)}), f32[16,8,128]{2,1,0:T(8,128)S(1)}, u32[]{:S(2)}, u32[]{:S(2)}) %all-to-all-start.1) | async-done | bytes 65568 | tf_op jit(solution)/shard_map/all_to_all | solution.py:945
  37.0 5.6 %fine.1 = (f32[9,16,4096]{2,1,0:T(8,128)}, f32[16,72,128]{2,1,0:T(8,128)}) custom-call(s32[32]{0:T(128)S(1)} %get-tuple-element.28.slot, f32[9,16,4096]{2,1,0:T(8,128)S(1)} %start.1.post, f32[16,8,128]{2,1,0:T(8,128)S(1)} %all-to-all-done.1.ghosts), custom_call_target="tpu_custom_call" | custom-call | tf_op jit(solution)/shard_map/fine/pallas_call | solution.py:946
  42.6 3.5 %all-to-all-start.2 = ((f32[16,72,128]{2,1,0:T(8,128)}), f32[16,72,128]{2,1,0:T(8,128)S(1)}, u32[]{:S(2)}, u32[]{:S(2)}) async-start(f32[16,72,128]{2,1,0:T(8,128)} %get-tuple-element.30.after), calls=%async_computation.2 | async-start | bytes 1179648 | tf_op jit(solution)/shard_map/all_to_all | solution.py:962
  46.2 10.9 %coarse.6 = (f32[9,1024,128]{2,1,0:T(8,128)}, f32[9,512,128]{2,1,0:T(8,128)S(1)}, s32[32]{0:T(128)S(1)}) custom-call(f32[9,1024,128]{2,1,0:T(8,128)} %coarse.7, f32[8,24,128]{2,1,0:T(8,128)S(1)} %all-to-all-done.asked, f32[1024,128]{1,0:T(8,128)} %get-tuple-element.27.inject_hbm, f32[16,72,128]{2,1,0:T(8,128)} %get-tuple-element.30.after, ...), custom_call_target="tpu_custom_call" | custom-call | tf_op jit(solution)/shard_map/coarse/pallas_call | solution.py:963
  57.0 5.6 %all-to-all-done.2.back = f32[16,72,128]{2,1,0:T(8,128)S(1)} async-done(((f32[16,72,128]{2,1,0:T(8,128)}), f32[16,72,128]{2,1,0:T(8,128)S(1)}, u32[]{:S(2)}, u32[]{:S(2)}) %all-to-all-start.2) | async-done | bytes 589856 | tf_op jit(solution)/shard_map/all_to_all | solution.py:962
  62.6 3.4 %patch.1 = (f32[9,512,128]{2,1,0:T(8,128)S(1)}, f32[9,1024,128]{2,1,0:T(8,128)}) custom-call(s32[16]{0:T(128)S(1)} %get-tuple-element.26.ids, s32[32]{0:T(128)S(1)} %get-tuple-element.31.home, f32[9,1024,128]{2,1,0:T(8,128)} %get-tuple-element.32.base, f32[9,512,128]{2,1,0:T(8,128)S(1)} %get-tuple-element.33.strips_in, ...), custom_call_target="tpu_custom_call", output_to_operand_aliasing={{1}: (2, {}), {0}: (3, {})} | custom-call | tf_op jit(solution)/shard_map/patch/pallas_call | solution.py:983
Async XLA Ops:
  2.2 14.4 %all-to-all-start = ((f32[8,24,128]{2,1,0:T(8,128)}), f32[8,24,128]{2,1,0:T(8,128)S(1)}, u32[]{:S(2)}, u32[]{:S(2)}) async-start(f32[8,24,128]{2,1,0:T(8,128)} %get-tuple-element.19), calls=%async_computation | async-start | bytes 196608 | tf_op jit(solution)/shard_map/all_to_all | solution.py:867
  13.4 5.2 %collective-permute-start = (f32[24,1024]{1,0:T(8,128)S(1)}, f32[24,1024]{1,0:T(8,128)S(1)}, u32[]{:S(2)}, u32[]{:S(2)}) collective-permute-start(f32[24,1024]{1,0:T(8,128)S(1)} %get-tuple-element.21), channel_id=1, source_target_pairs={{0,1},{1,2},{2,3},{3,0},{4,5},{5,6},{6,7},{7,4},{8,9},{9,10},{10,1... | collective-permute-start | bytes 294920 | tf_op jit(solution)/shard_map/ppermute | solution.py:873
  13.5 5.1 %collective-permute-start.1 = (f32[24,1024]{1,0:T(8,128)S(1)}, f32[24,1024]{1,0:T(8,128)S(1)}, u32[]{:S(2)}, u32[]{:S(2)}) collective-permute-start(f32[24,1024]{1,0:T(8,128)S(1)} %get-tuple-element.22), channel_id=1, source_target_pairs={{1,0},{2,1},{3,2},{0,3},{5,4},{6,5},{7,6},{4,7},{9,8},{10,9},{11,1... | collective-permute-start | bytes 294920 | tf_op jit(solution)/shard_map/ppermute | solution.py:874
  16.8 3.2 %collective-permute-start.2 = (f32[24,128]{1,0:T(8,128)S(1)}, f32[24,128]{1,0:T(8,128)S(1)}, u32[]{:S(2)}, u32[]{:S(2)}) collective-permute-start(f32[24,128]{1,0:T(8,128)S(1)} %get-tuple-element.24), channel_id=1, source_target_pairs={{0,1},{1,2},{2,3},{3,0},{4,5},{5,6},{6,7},{7,4},{8,9},{9,10},{10,1... | collective-permute-start | bytes 36872 | tf_op jit(solution)/shard_map/ppermute | solution.py:873
  16.9 3.1 %collective-permute-start.3 = (f32[24,128]{1,0:T(8,128)S(1)}, f32[24,128]{1,0:T(8,128)S(1)}, u32[]{:S(2)}, u32[]{:S(2)}) collective-permute-start(f32[24,128]{1,0:T(8,128)S(1)} %get-tuple-element.25), channel_id=1, source_target_pairs={{1,0},{2,1},{3,2},{0,3},{5,4},{6,5},{7,6},{4,7},{9,8},{10,9},{11,1... | collective-permute-start | bytes 36872 | tf_op jit(solution)/shard_map/ppermute | solution.py:874
  25.2 11.8 %all-to-all-start.1 = ((f32[16,8,128]{2,1,0:T(8,128)}), f32[16,8,128]{2,1,0:T(8,128)S(1)}, u32[]{:S(2)}, u32[]{:S(2)}) async-start(f32[16,8,128]{2,1,0:T(8,128)} %get-tuple-element.29), calls=%async_computation.1 | async-start | bytes 131072 | tf_op jit(solution)/shard_map/all_to_all | solution.py:945
  42.6 20.0 %all-to-all-start.2 = ((f32[16,72,128]{2,1,0:T(8,128)}), f32[16,72,128]{2,1,0:T(8,128)S(1)}, u32[]{:S(2)}, u32[]{:S(2)}) async-start(f32[16,72,128]{2,1,0:T(8,128)} %get-tuple-element.30.after), calls=%async_computation.2 | async-start | bytes 1179648 | tf_op jit(solution)/shard_map/all_to_all | solution.py:962

commit v3 on v2

--- a/solution.py
+++ b/solution.py
@@ -507,7 +507,9 @@
     lax.fori_loop(0, post.shape[2] // LANES, body, 0, unroll=2)
 
 
-def fine_kernel(slot, post, ghosts, fine, back, result, post_two, line, mean, swapped, sem):
+def fine_kernel(
+    slot, post, ghosts, fine, back_hbm, result, back, post_two, line, mean, swapped, sem, back_sem
+):
     places = post.shape[1]
     tiles = post.shape[2] // LANES
     tile = (8, LANES)
@@ -526,6 +528,10 @@
     def copy(q):
         target = fine.at[:, pl.ds(jnp.maximum(slot[q], 0), 1), :]
         return pltpu.make_async_copy(result.at[:, pl.ds(q, 1), :], target, sem.at[q])
+
+    def send(h):
+        part = pl.ds(8 * h, 8)
+        return pltpu.make_async_copy(back.at[part], back_hbm.at[part], back_sem.at[h])
 
     def half(h, carry):
         rows = pl.ds(pl.multiple_of(8 * h, 8), 8)
@@ -648,9 +654,12 @@
             flat = line.at[d]
             for q in range(8):
                 back[8 * h + q, d * 8 : d * 8 + 8, :] = flat[pl.ds(q, 8, stride=8), :]
+        send(h).start()
         return carry
 
     lax.fori_loop(0, places // 8, half, 0)
+    for h in range(places // 8):
+        send(h).wait()
     for q in range(places):
 
         @pl.when(slot[q] >= 0)
@@ -825,6 +834,10 @@
     return pltpu.with_memory_space_constraint(value, pltpu.HBM)
 
 
+def in_smem(value):
+    return pltpu.with_memory_space_constraint(value, pltpu.SMEM)
+
+
 def in_vmem(value):
     return pltpu.with_memory_space_constraint(value, pltpu.VMEM)
 
@@ -848,9 +861,12 @@
     def held(*shape):
         return pltpu.VMEM(shape, F32)
 
+    def table(size):
+        return pltpu.SMEM((size,), jnp.int32)
+
     ask, slot = pl.pallas_call(
         functools.partial(ask_kernel, columns, blocks_x, blocks_y, count_x),
-        out_shape=(held(count_x, 24, LANES), sds((2 * places,), jnp.int32)),
+        out_shape=(held(count_x, 24, LANES), table(2 * places)),
         in_specs=[hbm, hbm],
         out_specs=(vmem, smem),
         scratch_shapes=[
@@ -909,13 +925,13 @@
         scratch_shapes=[pltpu.SemaphoreType.DMA((places,))],
         name="start",
         compiler_params=GRANT,
-    )(slot, in_hbm(fine_turned))
+    )(in_smem(slot), in_hbm(fine_turned))
     message, inject, wanted = pl.pallas_call(
         functools.partial(ghost_kernel, count_x, count_y),
         out_shape=(
             held(places, 8, LANES),
             pltpu.HBM((width_x, LANES), F32),
-            sds((places,), jnp.int32),
+            table(places),
         ),
         in_specs=[hbm] + [vmem] * 7,
         out_specs=(vmem, hbm, smem),
@@ -945,29 +961,31 @@
     ghosts = in_vmem(lax.all_to_all(message, "gx", split_axis=0, concat_axis=0, tiled=True))
     fine_out, back = pl.pallas_call(
         fine_kernel,
-        out_shape=(pltpu.HBM((9, slots, cells), F32), held(places, 72, LANES)),
+        out_shape=(pltpu.HBM((9, slots, cells), F32), pltpu.HBM((places, 72, LANES), F32)),
         in_specs=[smem, vmem, vmem],
-        out_specs=(hbm, vmem),
+        out_specs=(hbm, hbm),
         scratch_shapes=[
             held(9, places, cells),
+            held(places, 72, LANES),
             held(9, 8, cells),
             held(9, 64, LANES),
             held(9, 8, 8, LANES),
             held(9, 8, 8, LANES),
             pltpu.SemaphoreType.DMA((places,)),
+            pltpu.SemaphoreType.DMA((places // 8,)),
         ],
         name="fine",
         compiler_params=GRANT,
-    )(slot, in_vmem(post), ghosts)
+    )(in_smem(slot), in_vmem(post), ghosts)
     returned = in_vmem(lax.all_to_all(back, "gx", split_axis=0, concat_axis=0, tiled=True))
     base, strips, home = pl.pallas_call(
         functools.partial(coarse_kernel, count_x, count_y),
         out_shape=(
             pltpu.HBM((9, width_x, width_y), F32),
             held(9, COARSE_EDGE * places, width_y),
-            sds((2 * places,), jnp.int32),
+            table(2 * places),
         ),
-        in_specs=[hbm, vmem, hbm, vmem, smem],
+        in_specs=[hbm, vmem, hbm, hbm, smem],
         out_specs=(hbm, vmem, smem),
         scratch_shapes=[
             held(width_x, LANES),
@@ -979,7 +997,7 @@
         ],
         name="coarse",
         compiler_params=GRANT,
-    )(in_hbm(coarse_pop), asked, in_hbm(inject), in_vmem(back), wanted)
+    )(in_hbm(coarse_pop), asked, in_hbm(inject), in_hbm(back), in_smem(wanted))
     _, coarse_out = pl.pallas_call(
         functools.partial(patch_kernel, blocks_y),
         out_shape=(
@@ -992,7 +1010,7 @@
         input_output_aliases={2: 1, 3: 0},
         name="patch",
         compiler_params=GRANT,
-    )(wanted, home, in_hbm(base), in_vmem(strips), returned)
+    )(in_smem(wanted), in_smem(home), in_hbm(base), in_vmem(strips), returned)
     return (coarse_out, jnp.transpose(fine_out, (1, 0, 2)))
 
 

time: 66.5 us -> 65.3 us (0.982)
  Pallas kernels: 34.2 us -> 30.8 us
  waiting for transfers between devices: 12 us -> 14.1 us
    pallas_call x1, Pallas kernels: 10.9 us -> 9.31 us  [local(): pl.pallas_call(functools.partial(coarse_kernel, count_x, count_y), out_sh...]
    all_to_all x1, waiting for transfers between devices: 5.55 us -> 7.11 us  [local(): lax.all_to_all(back, 'gx', split_axis=0, concat_axis=0, tiled=True)]
  transfers between devices with their start and end apart: 7 -> 7, of which waited for: 4 -> 4; matrix products, arithmetic and copies ran while one was open for 0% -> 0% of each run, Pallas kernels for 28% -> 25%
where the time goes in v3:
time: 65.3 us; the launch traced here: 64.8 us
  Pallas kernels  30.8 us (47%)
  starting transfers between devices  19.2 us (29%)
  waiting for transfers between devices  14.1 us (22%)
  between operations  0.71 us (1%)
    pallas_call x1, Pallas kernels, local(): pl.pallas_call(functools.partial(coarse_kernel, count_x, count_y), out_sh...  9.31 us
    all_to_all x1, starting transfers between devices, local(): lax.all_to_all(ask, 'gx', split_axis=0, concat_axis=0, tiled=True)  7.29 us
    all_to_all x1, waiting for transfers between devices, local(): lax.all_to_all(back, 'gx', split_axis=0, concat_axis=0, tiled=True)  7.11 us
    pallas_call x1, Pallas kernels, local(): pl.pallas_call(functools.partial(ghost_kernel, count_x, count_y), out_sha...  5.18 us
    pallas_call x1, Pallas kernels, local(): pl.pallas_call(fine_kernel, out_shape=(pltpu.HBM((9, slots, cells), F32),...  4.91 us
    all_to_all x1, starting transfers between devices, local(): lax.all_to_all(message, 'gx', split_axis=0, concat_axis=0, tiled=True)  4.73 us
    all_to_all x1, waiting for transfers between devices, local(): lax.all_to_all(message, 'gx', split_axis=0, concat_axis=0, tiled=True)  4.19 us
    pallas_call x1, Pallas kernels, local(): pl.pallas_call(pack_kernel, out_shape=(held(3, 9, 8, width_x), held(24, w...  3.93 us
  transfers between devices with their start and end apart: 7, of which 4 were waited for; matrix products, arithmetic and copies ran while one was open for 0% of the time, Pallas kernels for 25%

profile of v3, /device:TPU:0, one launch (start us, length us, event | category | flops | bytes accessed | tf_op | source)
XLA Modules:
  0.0 64.8 jit_solution(12006593956307252819)
XLA Ops:
  0.6 1.6 %ask.1 = (f32[8,24,128]{2,1,0:T(8,128)}, s32[32]{0:T(128)S(4)}) custom-call(s32[16]{0:T(128)} %block_hbm.1, f32[9,1024,128]{2,1,0:T(8,128)} %coarse.7), custom_call_target="tpu_custom_call" | custom-call | tf_op jit(solution)/shard_map/ask/pallas_call | solution.py:867
  2.2 7.3 %all-to-all-start = ((f32[8,24,128]{2,1,0:T(8,128)}), f32[8,24,128]{2,1,0:T(8,128)S(1)}, u32[]{:S(2)}, u32[]{:S(2)}) async-start(f32[8,24,128]{2,1,0:T(8,128)} %get-tuple-element.19), calls=%async_computation | async-start | bytes 196608 | tf_op jit(solution)/shard_map/all_to_all | solution.py:883
  9.5 3.9 %pack.1 = (f32[3,9,8,1024]{3,2,1,0:T(8,128)S(1)}, f32[24,1024]{1,0:T(8,128)S(1)}, f32[24,1024]{1,0:T(8,128)S(1)}) custom-call(f32[9,1024,128]{2,1,0:T(8,128)} %coarse.7), custom_call_target="tpu_custom_call" | custom-call | tf_op jit(solution)/shard_map/pack/pallas_call | solution.py:894
  13.4 0.1 collective-permute-start
  13.5 1.7 %collective-permute-start.1 = (f32[24,1024]{1,0:T(8,128)S(1)}, f32[24,1024]{1,0:T(8,128)S(1)}, u32[]{:S(2)}, u32[]{:S(2)}) collective-permute-start(f32[24,1024]{1,0:T(8,128)S(1)} %get-tuple-element.22), channel_id=1, source_target_pairs={{1,0},{2,1},{3,2},{0,3},{5,4},{6,5},{7,6},{4,7},{9,8},{10,9},{11,1... | collective-permute-start | bytes 294920 | tf_op jit(solution)/shard_map/ppermute | solution.py:890
  15.2 1.4 %all-to-all-done.asked = f32[8,24,128]{2,1,0:T(8,128)S(1)} async-done(((f32[8,24,128]{2,1,0:T(8,128)}), f32[8,24,128]{2,1,0:T(8,128)S(1)}, u32[]{:S(2)}, u32[]{:S(2)}) %all-to-all-start) | async-done | bytes 98336 | tf_op jit(solution)/shard_map/all_to_all | solution.py:883
  16.6 0.2 corner.1
  16.8 0.1 collective-permute-start.2
  16.9 1.7 %collective-permute-start.3 = (f32[24,128]{1,0:T(8,128)S(1)}, f32[24,128]{1,0:T(8,128)S(1)}, u32[]{:S(2)}, u32[]{:S(2)}) collective-permute-start(f32[24,128]{1,0:T(8,128)S(1)} %get-tuple-element.25), channel_id=1, source_target_pairs={{1,0},{2,1},{3,2},{0,3},{5,4},{6,5},{7,6},{4,7},{9,8},{10,9},{11,1... | collective-permute-start | bytes 36872 | tf_op jit(solution)/shard_map/ppermute | solution.py:890
  18.6 0.0 collective-permute-done.low_main
  18.6 0.0 collective-permute-done.1.high_main
  18.6 1.4 %collective-permute-done.2.low_ext = f32[24,128]{1,0:T(8,128)S(1)} collective-permute-done((f32[24,128]{1,0:T(8,128)S(1)}, f32[24,128]{1,0:T(8,128)S(1)}, u32[]{:S(2)}, u32[]{:S(2)}) %collective-permute-start.2) | collective-permute-done | bytes 12320 | tf_op jit(solution)/shard_map/ppermute | solution.py:889
  20.0 0.0 collective-permute-done.3.high_ext
  20.0 5.2 %ghost.1 = (f32[16,8,128]{2,1,0:T(8,128)}, f32[1024,128]{1,0:T(8,128)}, s32[16]{0:T(128)S(4)}) custom-call(f32[9,32,32,128]{3,2,1,0:T(8,128)} %bitcast.3, f32[8,24,128]{2,1,0:T(8,128)S(1)} %all-to-all-done.asked, f32[3,9,8,1024]{3,2,1,0:T(8,128)S(1)} %get-tuple-element.20.sets_main, f32[24,1024]{1,0:T(8,128)S(1)} %collective-permute-done.low_main, ...), custom_call_target="tpu_custom_call" | custom-call | tf_op jit(solution)/shard_map/ghost/pallas_call | solution.py:929
  25.2 4.7 %all-to-all-start.1 = ((f32[16,8,128]{2,1,0:T(8,128)}), f32[16,8,128]{2,1,0:T(8,128)S(1)}, u32[]{:S(2)}, u32[]{:S(2)}) async-start(f32[16,8,128]{2,1,0:T(8,128)} %get-tuple-element.29), calls=%async_computation.1 | async-start | bytes 131072 | tf_op jit(solution)/shard_map/all_to_all | solution.py:961
  29.9 2.9 %start.1.post = f32[9,16,4096]{2,1,0:T(8,128)S(1)} custom-call(s32[32]{0:T(128)S(4)} %get-tuple-element.28.slot, f32[9,16,4096]{2,1,0:T(8,128)} %bitcast.4), custom_call_target="tpu_custom_call" | custom-call | tf_op jit(solution)/shard_map/start/pallas_call | solution.py:920
  32.8 4.2 %all-to-all-done.1.ghosts = f32[16,8,128]{2,1,0:T(8,128)S(1)} async-done(((f32[16,8,128]{2,1,0:T(8,128)}), f32[16,8,128]{2,1,0:T(8,128)S(1)}, u32[]{:S(2)}, u32[]{:S(2)}) %all-to-all-start.1) | async-done | bytes 65568 | tf_op jit(solution)/shard_map/all_to_all | solution.py:961
  37.0 4.9 %fine.1 = (f32[9,16,4096]{2,1,0:T(8,128)}, f32[16,72,128]{2,1,0:T(8,128)}) custom-call(s32[32]{0:T(128)S(4)} %get-tuple-element.28.slot, f32[9,16,4096]{2,1,0:T(8,128)S(1)} %start.1.post, f32[16,8,128]{2,1,0:T(8,128)S(1)} %all-to-all-done.1.ghosts), custom_call_target="tpu_custom_call" | custom-call | tf_op jit(solution)/shard_map/fine/pallas_call | solution.py:962
  41.9 3.5 %all-to-all-start.2 = ((f32[16,72,128]{2,1,0:T(8,128)}), f32[16,72,128]{2,1,0:T(8,128)S(1)}, u32[]{:S(2)}, u32[]{:S(2)}) async-start(f32[16,72,128]{2,1,0:T(8,128)} %get-tuple-element.30.after), calls=%async_computation.2 | async-start | bytes 1179648 | tf_op jit(solution)/shard_map/all_to_all | solution.py:980
  45.5 9.3 %coarse.6 = (f32[9,1024,128]{2,1,0:T(8,128)}, f32[9,512,128]{2,1,0:T(8,128)S(1)}, s32[32]{0:T(128)S(4)}) custom-call(f32[9,1024,128]{2,1,0:T(8,128)} %coarse.7, f32[8,24,128]{2,1,0:T(8,128)S(1)} %all-to-all-done.asked, f32[1024,128]{1,0:T(8,128)} %get-tuple-element.27.inject_hbm, f32[16,72,128]{2,1,0:T(8,128)} %get-tuple-element.30.after, ...), custom_call_target="tpu_custom_call" | custom-call | tf_op jit(solution)/shard_map/coarse/pallas_call | solution.py:981
  54.8 7.1 %all-to-all-done.2.back = f32[16,72,128]{2,1,0:T(8,128)S(1)} async-done(((f32[16,72,128]{2,1,0:T(8,128)}), f32[16,72,128]{2,1,0:T(8,128)S(1)}, u32[]{:S(2)}, u32[]{:S(2)}) %all-to-all-start.2) | async-done | bytes 589856 | tf_op jit(solution)/shard_map/all_to_all | solution.py:980
  61.9 2.9 %patch.1 = (f32[9,512,128]{2,1,0:T(8,128)S(1)}, f32[9,1024,128]{2,1,0:T(8,128)}) custom-call(s32[16]{0:T(128)S(4)} %get-tuple-element.26.ids, s32[32]{0:T(128)S(4)} %get-tuple-element.31.home, f32[9,1024,128]{2,1,0:T(8,128)} %get-tuple-element.32.base, f32[9,512,128]{2,1,0:T(8,128)S(1)} %get-tuple-element.33.strips_in, ...), custom_call_target="tpu_custom_call", output_to_operand_aliasing={{1}: (2, {}), {0}: (3, {})} | custom-call | tf_op jit(solution)/shard_map/patch/pallas_call | solution.py:1001
Async XLA Ops:
  2.2 14.4 %all-to-all-start = ((f32[8,24,128]{2,1,0:T(8,128)}), f32[8,24,128]{2,1,0:T(8,128)S(1)}, u32[]{:S(2)}, u32[]{:S(2)}) async-start(f32[8,24,128]{2,1,0:T(8,128)} %get-tuple-element.19), calls=%async_computation | async-start | bytes 196608 | tf_op jit(solution)/shard_map/all_to_all | solution.py:883
  13.4 5.2 %collective-permute-start = (f32[24,1024]{1,0:T(8,128)S(1)}, f32[24,1024]{1,0:T(8,128)S(1)}, u32[]{:S(2)}, u32[]{:S(2)}) collective-permute-start(f32[24,1024]{1,0:T(8,128)S(1)} %get-tuple-element.21), channel_id=1, source_target_pairs={{0,1},{1,2},{2,3},{3,0},{4,5},{5,6},{6,7},{7,4},{8,9},{9,10},{10,1... | collective-permute-start | bytes 294920 | tf_op jit(solution)/shard_map/ppermute | solution.py:889
  13.5 5.1 %collective-permute-start.1 = (f32[24,1024]{1,0:T(8,128)S(1)}, f32[24,1024]{1,0:T(8,128)S(1)}, u32[]{:S(2)}, u32[]{:S(2)}) collective-permute-start(f32[24,1024]{1,0:T(8,128)S(1)} %get-tuple-element.22), channel_id=1, source_target_pairs={{1,0},{2,1},{3,2},{0,3},{5,4},{6,5},{7,6},{4,7},{9,8},{10,9},{11,1... | collective-permute-start | bytes 294920 | tf_op jit(solution)/shard_map/ppermute | solution.py:890
  16.8 3.2 %collective-permute-start.2 = (f32[24,128]{1,0:T(8,128)S(1)}, f32[24,128]{1,0:T(8,128)S(1)}, u32[]{:S(2)}, u32[]{:S(2)}) collective-permute-start(f32[24,128]{1,0:T(8,128)S(1)} %get-tuple-element.24), channel_id=1, source_target_pairs={{0,1},{1,2},{2,3},{3,0},{4,5},{5,6},{6,7},{7,4},{8,9},{9,10},{10,1... | collective-permute-start | bytes 36872 | tf_op jit(solution)/shard_map/ppermute | solution.py:889
  16.9 3.1 %collective-permute-start.3 = (f32[24,128]{1,0:T(8,128)S(1)}, f32[24,128]{1,0:T(8,128)S(1)}, u32[]{:S(2)}, u32[]{:S(2)}) collective-permute-start(f32[24,128]{1,0:T(8,128)S(1)} %get-tuple-element.25), channel_id=1, source_target_pairs={{1,0},{2,1},{3,2},{0,3},{5,4},{6,5},{7,6},{4,7},{9,8},{10,9},{11,1... | collective-permute-start | bytes 36872 | tf_op jit(solution)/shard_map/ppermute | solution.py:890
  25.2 11.8 %all-to-all-start.1 = ((f32[16,8,128]{2,1,0:T(8,128)}), f32[16,8,128]{2,1,0:T(8,128)S(1)}, u32[]{:S(2)}, u32[]{:S(2)}) async-start(f32[16,8,128]{2,1,0:T(8,128)} %get-tuple-element.29), calls=%async_computation.1 | async-start | bytes 131072 | tf_op jit(solution)/shard_map/all_to_all | solution.py:961
  41.9 20.0 %all-to-all-start.2 = ((f32[16,72,128]{2,1,0:T(8,128)}), f32[16,72,128]{2,1,0:T(8,128)S(1)}, u32[]{:S(2)}, u32[]{:S(2)}) async-start(f32[16,72,128]{2,1,0:T(8,128)} %get-tuple-element.30.after), calls=%async_computation.2 | async-start | bytes 1179648 | tf_op jit(solution)/shard_map/all_to_all | solution.py:980

commit v4 on v3

--- a/solution.py
+++ b/solution.py
@@ -110,7 +110,8 @@
     for place in range(places):
         id_ref[place] = -1
         slot_ref[place] = -1
-        slot_ref[places + place] = 0
+        for part in range(1, 4):
+            slot_ref[part * places + place] = 0
     for owner in range(count_x):
         seen_ref[owner] = 0
     blocks.wait()
@@ -125,6 +126,8 @@
         id_ref[place] = (column - owner * blocks_x) * blocks_y + lax.rem(row, blocks_y)
         slot_ref[place] = slot
         slot_ref[places + place] = jnp.where(row == 0, 1, 0) + jnp.where(row == columns - 1, 2, 0)
+        slot_ref[2 * places + place] = lax.rem(row * COARSE_EDGE, LANES)
+        slot_ref[3 * places + place] = lax.rem(column * COARSE_EDGE, LANES)
     rows[...] = jnp.full(rows.shape, 0.1, F32)
     for copy in copies:
         copy.wait()
@@ -213,26 +216,21 @@
     turn_columns(z, sets, to_high, to_low)
 
 
-def window(parts, j, off):
+def turned(part, j):
+    return pltpu.roll(part, WINDOW * j, 1) if j else part
+
+
+def windows(parts, off):
     lane = lane_of((8, LANES))
-    before, value, after = parts
-    shift = (WINDOW * j - off + 1) % LANES
-
-    def move(part):
-        return pltpu.roll(part, shift, 1) if shift else part
-
-    value = move(value)
-    if off == 0:
-        value = jnp.where(lane == WINDOW * j, move(before), value)
-    if off == LANES - COARSE_EDGE:
-        value = jnp.where(lane == WINDOW * j + COARSE_EDGE + 1, move(after), value)
-    return value
-
-
-def join(parts):
-    lane = lane_of((8, LANES))
-    first, second, third = parts
-    return jnp.where(lane < WINDOW, first, jnp.where(lane < 2 * WINDOW, second, third))
+    got = []
+    for j, (before, value, after) in enumerate(parts):
+        if off == 0:
+            value = jnp.where(lane == (WINDOW * j - 1) % LANES, before, value)
+        if off == LANES - COARSE_EDGE:
+            value = jnp.where(lane == WINDOW * j, after, value)
+        got.append(value)
+    place = (lane - (off - 1)) & (LANES - 1)
+    return jnp.where(place < WINDOW, got[0], jnp.where(place < 2 * WINDOW, got[1], got[2]))
 
 
 def ghost_kernel(
@@ -354,14 +352,14 @@
 
     lax.fori_loop(0, tiles, ghosts_t, 0)
     for sub in range(2):
+        moved = [
+            [turned(g_t[sub, j, :, LANES * k : LANES * (k + 1)], j) for k in range(tiles)]
+            for j in range(3)
+        ]
         for bx in range(blocks_x):
             t, off = divmod(COARSE_EDGE * bx, LANES)
-            near = [(t + step) % tiles for step in (-1, 0, 1)]
-            got = []
-            for j in range(3):
-                parts = [g_t[sub, j, :, LANES * k : LANES * (k + 1)] for k in near]
-                got.append(window(parts, j, off))
-            pack_t[sub, bx] = join(got)
+            parts = [(m[t - 1], m[t], m[t + 1]) for m in moved]
+            pack_t[sub, bx] = windows(parts, off)
 
     plane = (blocks_x, LANES)
     rows_b = row_of(plane)
@@ -453,13 +451,13 @@
         rows = pl.ds(pl.multiple_of(k * 8, 8), 8)
         for side in range(2):
             for sub in range(2):
+                parts = []
+                for j in range(3):
+                    one = turned(g_r[side, j, sub, rows, 0:LANES], j)
+                    two = turned(g_r[side, j, sub, rows, LANES:], j)
+                    parts.append((two, one, two))
                 for by in range(blocks_y):
-                    got = []
-                    for j in range(3):
-                        one = g_r[side, j, sub, rows, 0:LANES]
-                        two = g_r[side, j, sub, rows, LANES:]
-                        got.append(window((two, one, two), j, COARSE_EDGE * by))
-                    pack_r[side, sub, by, rows, :] = join(got)
+                    pack_r[side, sub, by, rows, :] = windows(parts, COARSE_EDGE * by)
         return carry
 
     lax.fori_loop(0, blocks_x // 8, windows_r, 0)
@@ -480,7 +478,7 @@
                 message[q, row : row + 1, :] = pack_t[sub, bx, pl.ds(4 * side + by, 1), :]
         return carry
 
-    lax.fori_loop(0, message.shape[0], pick, 0)
+    lax.fori_loop(0, message.shape[0], pick, 0, unroll=4)
     copy_inject.wait()
 
 
@@ -523,7 +521,6 @@
     turn_back = jnp.where(even, lane, (lane - 63) & (LANES - 1))
     cell = (turn_back & 63) + (turn_back >> 6)
     along = [(WINDOW * j + 1 + ((cell - c) >> 1)) & (LANES - 1) for j, c in enumerate(ORDER)]
-    squeeze = 64 * ((lane >> 5) & 1) + 2 * (lane & 31) + (lane >> 6)
 
     def copy(q):
         target = fine.at[:, pl.ds(jnp.maximum(slot[q], 0), 1), :]
@@ -536,8 +533,16 @@
     def half(h, carry):
         rows = pl.ds(pl.multiple_of(8 * h, 8), 8)
         wall = jnp.zeros(tile, jnp.int32)
+        off_y, off_x = wall, wall
         for r in range(8):
-            wall = jnp.where(row == r, slot[places + 8 * h + r], wall)
+            here = row == r
+            wall = jnp.where(here, slot[places + 8 * h + r], wall)
+            off_y = jnp.where(here, slot[2 * places + 8 * h + r], off_y)
+            off_x = jnp.where(here, slot[3 * places + 8 * h + r], off_x)
+        over_own = [(index + off_y - 1) & (LANES - 1) for index in over]
+        along_own = [(index + off_x - 1) & (LANES - 1) for index in along]
+        quarter = ((lane >> 5) - (off_y >> 5)) & 3
+        squeeze = 64 * (quarter & 1) + 2 * (lane & 31) + (quarter >> 1)
         wall_low = at_low & ((wall & 1) != 0)
         wall_high = at_high & ((wall & 2) != 0)
 
@@ -545,10 +550,12 @@
             border = [
                 ghosts2[pl.ds(h * 64 + 4 * sub + side, 8, stride=8), :] for side in range(4)
             ]
-            up = [take_lanes(border[0], over[j]) for j in range(3)]
-            down = [take_lanes(border[1], over[j]) for j in range(3)]
+            up = [take_lanes(border[0], over_own[j]) for j in range(3)]
+            down = [take_lanes(border[1], over_own[j]) for j in range(3)]
             beside = [
-                jnp.where(even, take_lanes(border[2], along[j]), take_lanes(border[3], along[j]))
+                jnp.where(
+                    even, take_lanes(border[2], along_own[j]), take_lanes(border[3], along_own[j])
+                )
                 for j in range(3)
             ]
 
@@ -807,7 +814,7 @@
                 for d in group:
                     value = back[q, d * 8 : d * 8 + 8, :]
                     for j in range(4):
-                        moved = pltpu.roll(value, lax.rem(by + 4 - j, 4) * 32, 1)
+                        moved = pltpu.roll(value, LANES - 32 * j, 1) if j else value
                         merged.append((d, pl.ds(start + 8 * j, 8), moved))
                 merged = [
                     (d, rows, jnp.where(inside, moved, strips[d, rows, :]))
@@ -866,7 +873,7 @@
 
     ask, slot = pl.pallas_call(
         functools.partial(ask_kernel, columns, blocks_x, blocks_y, count_x),
-        out_shape=(held(count_x, 24, LANES), table(2 * places)),
+        out_shape=(held(count_x, 24, LANES), table(4 * places)),
         in_specs=[hbm, hbm],
         out_specs=(vmem, smem),
         scratch_shapes=[

time: 65.3 us -> 64.7 us (level)
  no operation moved by 1% of the time
where the time goes in v4:
time: 64.7 us; the launch traced here: 64.2 us
  Pallas kernels  30.3 us (47%)
  starting transfers between devices  19.1 us (30%)
  waiting for transfers between devices  14.1 us (22%)
  between operations  0.71 us (1%)
    pallas_call x1, Pallas kernels, local(): pl.pallas_call(functools.partial(coarse_kernel, count_x, count_y), out_sh...  9.31 us
    all_to_all x1, starting transfers between devices, local(): lax.all_to_all(ask, 'gx', split_axis=0, concat_axis=0, tiled=True)  7.29 us
    all_to_all x1, waiting for transfers between devices, local(): lax.all_to_all(back, 'gx', split_axis=0, concat_axis=0, tiled=True)  7.11 us
    pallas_call x1, Pallas kernels, local(): pl.pallas_call(fine_kernel, out_shape=(pltpu.HBM((9, slots, cells), F32),...  4.93 us
    pallas_call x1, Pallas kernels, local(): pl.pallas_call(functools.partial(ghost_kernel, count_x, count_y), out_sha...  4.87 us
    all_to_all x1, starting transfers between devices, local(): lax.all_to_all(message, 'gx', split_axis=0, concat_axis=0, tiled=True)  4.73 us
    all_to_all x1, waiting for transfers between devices, local(): lax.all_to_all(message, 'gx', split_axis=0, concat_axis=0, tiled=True)  4.19 us
    pallas_call x1, Pallas kernels, local(): pl.pallas_call(pack_kernel, out_shape=(held(3, 9, 8, width_x), held(24, w...  3.93 us
  transfers between devices with their start and end apart: 7, of which 4 were waited for; matrix products, arithmetic and copies ran while one was open for 0% of the time, Pallas kernels for 25%

profile of v4, /device:TPU:0, one launch (start us, length us, event | category | flops | bytes accessed | tf_op | source)
XLA Modules:
  0.0 64.2 jit_solution(17804066200902264217)
XLA Ops:
  0.6 1.6 %ask.1 = (f32[8,24,128]{2,1,0:T(8,128)}, s32[64]{0:T(128)S(4)}) custom-call(s32[16]{0:T(128)} %block_hbm.1, f32[9,1024,128]{2,1,0:T(8,128)} %coarse.7), custom_call_target="tpu_custom_call" | custom-call | tf_op jit(solution)/shard_map/ask/pallas_call | solution.py:874
  2.3 7.3 %all-to-all-start = ((f32[8,24,128]{2,1,0:T(8,128)}), f32[8,24,128]{2,1,0:T(8,128)S(1)}, u32[]{:S(2)}, u32[]{:S(2)}) async-start(f32[8,24,128]{2,1,0:T(8,128)} %get-tuple-element.19), calls=%async_computation | async-start | bytes 196608 | tf_op jit(solution)/shard_map/all_to_all | solution.py:890
  9.6 3.9 %pack.1 = (f32[3,9,8,1024]{3,2,1,0:T(8,128)S(1)}, f32[24,1024]{1,0:T(8,128)S(1)}, f32[24,1024]{1,0:T(8,128)S(1)}) custom-call(f32[9,1024,128]{2,1,0:T(8,128)} %coarse.7), custom_call_target="tpu_custom_call" | custom-call | tf_op jit(solution)/shard_map/pack/pallas_call | solution.py:901
  13.5 0.1 collective-permute-start
  13.6 1.7 %collective-permute-start.1 = (f32[24,1024]{1,0:T(8,128)S(1)}, f32[24,1024]{1,0:T(8,128)S(1)}, u32[]{:S(2)}, u32[]{:S(2)}) collective-permute-start(f32[24,1024]{1,0:T(8,128)S(1)} %get-tuple-element.22), channel_id=1, source_target_pairs={{1,0},{2,1},{3,2},{0,3},{5,4},{6,5},{7,6},{4,7},{9,8},{10,9},{11,1... | collective-permute-start | bytes 294920 | tf_op jit(solution)/shard_map/ppermute | solution.py:897
  15.3 1.4 %all-to-all-done.asked = f32[8,24,128]{2,1,0:T(8,128)S(1)} async-done(((f32[8,24,128]{2,1,0:T(8,128)}), f32[8,24,128]{2,1,0:T(8,128)S(1)}, u32[]{:S(2)}, u32[]{:S(2)}) %all-to-all-start) | async-done | bytes 98336 | tf_op jit(solution)/shard_map/all_to_all | solution.py:890
  16.7 0.2 corner.1
  16.9 0.1 collective-permute-start.2
  16.9 1.7 %collective-permute-start.3 = (f32[24,128]{1,0:T(8,128)S(1)}, f32[24,128]{1,0:T(8,128)S(1)}, u32[]{:S(2)}, u32[]{:S(2)}) collective-permute-start(f32[24,128]{1,0:T(8,128)S(1)} %get-tuple-element.25), channel_id=1, source_target_pairs={{1,0},{2,1},{3,2},{0,3},{5,4},{6,5},{7,6},{4,7},{9,8},{10,9},{11,1... | collective-permute-start | bytes 36872 | tf_op jit(solution)/shard_map/ppermute | solution.py:897
  18.7 0.0 collective-permute-done.low_main
  18.7 0.0 collective-permute-done.1.high_main
  18.7 1.4 %collective-permute-done.2.low_ext = f32[24,128]{1,0:T(8,128)S(1)} collective-permute-done((f32[24,128]{1,0:T(8,128)S(1)}, f32[24,128]{1,0:T(8,128)S(1)}, u32[]{:S(2)}, u32[]{:S(2)}) %collective-permute-start.2) | collective-permute-done | bytes 12320 | tf_op jit(solution)/shard_map/ppermute | solution.py:896
  20.1 0.0 collective-permute-done.3.high_ext
  20.1 4.9 %ghost.1 = (f32[16,8,128]{2,1,0:T(8,128)}, f32[1024,128]{1,0:T(8,128)}, s32[16]{0:T(128)S(4)}) custom-call(f32[9,32,32,128]{3,2,1,0:T(8,128)} %bitcast.3, f32[8,24,128]{2,1,0:T(8,128)S(1)} %all-to-all-done.asked, f32[3,9,8,1024]{3,2,1,0:T(8,128)S(1)} %get-tuple-element.20.sets_main, f32[24,1024]{1,0:T(8,128)S(1)} %collective-permute-done.low_main, ...), custom_call_target="tpu_custom_call" | custom-call | tf_op jit(solution)/shard_map/ghost/pallas_call | solution.py:936
  25.0 4.7 %all-to-all-start.1 = ((f32[16,8,128]{2,1,0:T(8,128)}), f32[16,8,128]{2,1,0:T(8,128)S(1)}, u32[]{:S(2)}, u32[]{:S(2)}) async-start(f32[16,8,128]{2,1,0:T(8,128)} %get-tuple-element.29), calls=%async_computation.1 | async-start | bytes 131072 | tf_op jit(solution)/shard_map/all_to_all | solution.py:968
  29.7 2.9 %start.1.post = f32[9,16,4096]{2,1,0:T(8,128)S(1)} custom-call(s32[64]{0:T(128)S(4)} %get-tuple-element.28.slot, f32[9,16,4096]{2,1,0:T(8,128)} %bitcast.4), custom_call_target="tpu_custom_call" | custom-call | tf_op jit(solution)/shard_map/start/pallas_call | solution.py:927
  32.6 4.2 %all-to-all-done.1.ghosts = f32[16,8,128]{2,1,0:T(8,128)S(1)} async-done(((f32[16,8,128]{2,1,0:T(8,128)}), f32[16,8,128]{2,1,0:T(8,128)S(1)}, u32[]{:S(2)}, u32[]{:S(2)}) %all-to-all-start.1) | async-done | bytes 65568 | tf_op jit(solution)/shard_map/all_to_all | solution.py:968
  36.8 4.9 %fine.1 = (f32[9,16,4096]{2,1,0:T(8,128)}, f32[16,72,128]{2,1,0:T(8,128)}) custom-call(s32[64]{0:T(128)S(4)} %get-tuple-element.28.slot, f32[9,16,4096]{2,1,0:T(8,128)S(1)} %start.1.post, f32[16,8,128]{2,1,0:T(8,128)S(1)} %all-to-all-done.1.ghosts), custom_call_target="tpu_custom_call" | custom-call | tf_op jit(solution)/shard_map/fine/pallas_call | solution.py:969
  41.7 3.5 %all-to-all-start.2 = ((f32[16,72,128]{2,1,0:T(8,128)}), f32[16,72,128]{2,1,0:T(8,128)S(1)}, u32[]{:S(2)}, u32[]{:S(2)}) async-start(f32[16,72,128]{2,1,0:T(8,128)} %get-tuple-element.30.after), calls=%async_computation.2 | async-start | bytes 1179648 | tf_op jit(solution)/shard_map/all_to_all | solution.py:987
  45.3 9.3 %coarse.6 = (f32[9,1024,128]{2,1,0:T(8,128)}, f32[9,512,128]{2,1,0:T(8,128)S(1)}, s32[32]{0:T(128)S(4)}) custom-call(f32[9,1024,128]{2,1,0:T(8,128)} %coarse.7, f32[8,24,128]{2,1,0:T(8,128)S(1)} %all-to-all-done.asked, f32[1024,128]{1,0:T(8,128)} %get-tuple-element.27.inject_hbm, f32[16,72,128]{2,1,0:T(8,128)} %get-tuple-element.30.after, ...), custom_call_target="tpu_custom_call" | custom-call | tf_op jit(solution)/shard_map/coarse/pallas_call | solution.py:988
  54.6 7.1 %all-to-all-done.2.back = f32[16,72,128]{2,1,0:T(8,128)S(1)} async-done(((f32[16,72,128]{2,1,0:T(8,128)}), f32[16,72,128]{2,1,0:T(8,128)S(1)}, u32[]{:S(2)}, u32[]{:S(2)}) %all-to-all-start.2) | async-done | bytes 589856 | tf_op jit(solution)/shard_map/all_to_all | solution.py:987
  61.7 2.5 %patch.1 = (f32[9,512,128]{2,1,0:T(8,128)S(1)}, f32[9,1024,128]{2,1,0:T(8,128)}) custom-call(s32[16]{0:T(128)S(4)} %get-tuple-element.26.ids, s32[32]{0:T(128)S(4)} %get-tuple-element.31.home, f32[9,1024,128]{2,1,0:T(8,128)} %get-tuple-element.32.base, f32[9,512,128]{2,1,0:T(8,128)S(1)} %get-tuple-element.33.strips_in, ...), custom_call_target="tpu_custom_call", output_to_operand_aliasing={{1}: (2, {}), {0}: (3, {})} | custom-call | tf_op jit(solution)/shard_map/patch/pallas_call | solution.py:1008
Async XLA Ops:
  2.3 14.4 %all-to-all-start = ((f32[8,24,128]{2,1,0:T(8,128)}), f32[8,24,128]{2,1,0:T(8,128)S(1)}, u32[]{:S(2)}, u32[]{:S(2)}) async-start(f32[8,24,128]{2,1,0:T(8,128)} %get-tuple-element.19), calls=%async_computation | async-start | bytes 196608 | tf_op jit(solution)/shard_map/all_to_all | solution.py:890
  13.5 5.2 %collective-permute-start = (f32[24,1024]{1,0:T(8,128)S(1)}, f32[24,1024]{1,0:T(8,128)S(1)}, u32[]{:S(2)}, u32[]{:S(2)}) collective-permute-start(f32[24,1024]{1,0:T(8,128)S(1)} %get-tuple-element.21), channel_id=1, source_target_pairs={{0,1},{1,2},{2,3},{3,0},{4,5},{5,6},{6,7},{7,4},{8,9},{9,10},{10,1... | collective-permute-start | bytes 294920 | tf_op jit(solution)/shard_map/ppermute | solution.py:896
  13.6 5.1 %collective-permute-start.1 = (f32[24,1024]{1,0:T(8,128)S(1)}, f32[24,1024]{1,0:T(8,128)S(1)}, u32[]{:S(2)}, u32[]{:S(2)}) collective-permute-start(f32[24,1024]{1,0:T(8,128)S(1)} %get-tuple-element.22), channel_id=1, source_target_pairs={{1,0},{2,1},{3,2},{0,3},{5,4},{6,5},{7,6},{4,7},{9,8},{10,9},{11,1... | collective-permute-start | bytes 294920 | tf_op jit(solution)/shard_map/ppermute | solution.py:897
  16.9 3.2 %collective-permute-start.2 = (f32[24,128]{1,0:T(8,128)S(1)}, f32[24,128]{1,0:T(8,128)S(1)}, u32[]{:S(2)}, u32[]{:S(2)}) collective-permute-start(f32[24,128]{1,0:T(8,128)S(1)} %get-tuple-element.24), channel_id=1, source_target_pairs={{0,1},{1,2},{2,3},{3,0},{4,5},{5,6},{6,7},{7,4},{8,9},{9,10},{10,1... | collective-permute-start | bytes 36872 | tf_op jit(solution)/shard_map/ppermute | solution.py:896
  16.9 3.1 %collective-permute-start.3 = (f32[24,128]{1,0:T(8,128)S(1)}, f32[24,128]{1,0:T(8,128)S(1)}, u32[]{:S(2)}, u32[]{:S(2)}) collective-permute-start(f32[24,128]{1,0:T(8,128)S(1)} %get-tuple-element.25), channel_id=1, source_target_pairs={{1,0},{2,1},{3,2},{0,3},{5,4},{6,5},{7,6},{4,7},{9,8},{10,9},{11,1... | collective-permute-start | bytes 36872 | tf_op jit(solution)/shard_map/ppermute | solution.py:897
  25.0 11.8 %all-to-all-start.1 = ((f32[16,8,128]{2,1,0:T(8,128)}), f32[16,8,128]{2,1,0:T(8,128)S(1)}, u32[]{:S(2)}, u32[]{:S(2)}) async-start(f32[16,8,128]{2,1,0:T(8,128)} %get-tuple-element.29), calls=%async_computation.1 | async-start | bytes 131072 | tf_op jit(solution)/shard_map/all_to_all | solution.py:968
  41.7 20.0 %all-to-all-start.2 = ((f32[16,72,128]{2,1,0:T(8,128)}), f32[16,72,128]{2,1,0:T(8,128)S(1)}, u32[]{:S(2)}, u32[]{:S(2)}) async-start(f32[16,72,128]{2,1,0:T(8,128)} %get-tuple-element.30.after), calls=%async_computation.2 | async-start | bytes 1179648 | tf_op jit(solution)/shard_map/all_to_all | solution.py:987

commit v5 on v4

--- a/solution.py
+++ b/solution.py
@@ -317,7 +317,7 @@
         collide_tile(sets_main, low_main, high_main, lanes, lanes)
         return carry
 
-    lax.fori_loop(0, tiles - 1, collide_t, 0)
+    lax.fori_loop(0, tiles - 1, collide_t, 0, unroll=2)
     collide_tile(sets_ext, low_ext, high_ext, pl.ds(0, LANES), pl.ds(width, LANES))
     turn[...] = jnp.zeros(turn.shape, F32)
     row_t = row_of((8, wide))
@@ -350,7 +350,7 @@
                 g_t[sub, j, :, lanes] = jnp.where(row8 < 4, out[LEFT[j]], out[RIGHT[j]])
         return carry
 
-    lax.fori_loop(0, tiles, ghosts_t, 0)
+    lax.fori_loop(0, tiles, ghosts_t, 0, unroll=3)
     for sub in range(2):
         moved = [
             [turned(g_t[sub, j, :, LANES * k : LANES * (k + 1)], j) for k in range(tiles)]
@@ -407,7 +407,7 @@
             raw_r[k, d, :, LANES:] = pltpu.roll(far[k], lax.rem(LANES - 4 * d, LANES), 1)
         return carry
 
-    lax.fori_loop(0, 9, raw_rows, 0)
+    lax.fori_loop(0, 9, raw_rows, 0, unroll=3)
 
     def collide_r(k, carry):
         rows = pl.ds(pl.multiple_of(k * 8, 8), 8)

time: 64.7 us -> 64.3 us (level)
  transfers between devices with their start and end apart: 7 -> 7, of which waited for: 4 -> 4; matrix products, arithmetic and copies ran while one was open for 0% -> 0% of each run, Pallas kernels for 25% -> 26%
where the time goes in v5:
time: 64.3 us; the launch traced here: 63.8 us
  Pallas kernels  29.9 us (47%)
  starting transfers between devices  19.2 us (30%)
  waiting for transfers between devices  14.1 us (22%)
  between operations  0.71 us (1%)
    pallas_call x1, Pallas kernels, local(): pl.pallas_call(functools.partial(coarse_kernel, count_x, count_y), out_sh...  9.31 us
    all_to_all x1, starting transfers between devices, local(): lax.all_to_all(ask, 'gx', split_axis=0, concat_axis=0, tiled=True)  7.29 us
    all_to_all x1, waiting for transfers between devices, local(): lax.all_to_all(back, 'gx', split_axis=0, concat_axis=0, tiled=True)  7.11 us
    pallas_call x1, Pallas kernels, local(): pl.pallas_call(fine_kernel, out_shape=(pltpu.HBM((9, slots, cells), F32),...  4.93 us
    all_to_all x1, starting transfers between devices, local(): lax.all_to_all(message, 'gx', split_axis=0, concat_axis=0, tiled=True)  4.73 us
    pallas_call x1, Pallas kernels, local(): pl.pallas_call(functools.partial(ghost_kernel, count_x, count_y), out_sha...  4.49 us
    all_to_all x1, waiting for transfers between devices, local(): lax.all_to_all(message, 'gx', split_axis=0, concat_axis=0, tiled=True)  4.19 us
    pallas_call x1, Pallas kernels, local(): pl.pallas_call(pack_kernel, out_shape=(held(3, 9, 8, width_x), held(24, w...  3.93 us
  transfers between devices with their start and end apart: 7, of which 4 were waited for; matrix products, arithmetic and copies ran while one was open for 0% of the time, Pallas kernels for 26%

profile of v5, /device:TPU:0, one launch (start us, length us, event | category | flops | bytes accessed | tf_op | source)
XLA Modules:
  0.0 63.8 jit_solution(3749010864390180560)
XLA Ops:
  0.6 1.6 %ask.1 = (f32[8,24,128]{2,1,0:T(8,128)}, s32[64]{0:T(128)S(4)}) custom-call(s32[16]{0:T(128)} %block_hbm.1, f32[9,1024,128]{2,1,0:T(8,128)} %coarse.7), custom_call_target="tpu_custom_call" | custom-call | tf_op jit(solution)/shard_map/ask/pallas_call | solution.py:874
  2.3 7.3 %all-to-all-start = ((f32[8,24,128]{2,1,0:T(8,128)}), f32[8,24,128]{2,1,0:T(8,128)S(1)}, u32[]{:S(2)}, u32[]{:S(2)}) async-start(f32[8,24,128]{2,1,0:T(8,128)} %get-tuple-element.19), calls=%async_computation | async-start | bytes 196608 | tf_op jit(solution)/shard_map/all_to_all | solution.py:890
  9.6 3.9 %pack.1 = (f32[3,9,8,1024]{3,2,1,0:T(8,128)S(1)}, f32[24,1024]{1,0:T(8,128)S(1)}, f32[24,1024]{1,0:T(8,128)S(1)}) custom-call(f32[9,1024,128]{2,1,0:T(8,128)} %coarse.7), custom_call_target="tpu_custom_call" | custom-call | tf_op jit(solution)/shard_map/pack/pallas_call | solution.py:901
  13.5 0.1 collective-permute-start
  13.6 1.7 %collective-permute-start.1 = (f32[24,1024]{1,0:T(8,128)S(1)}, f32[24,1024]{1,0:T(8,128)S(1)}, u32[]{:S(2)}, u32[]{:S(2)}) collective-permute-start(f32[24,1024]{1,0:T(8,128)S(1)} %get-tuple-element.22), channel_id=1, source_target_pairs={{1,0},{2,1},{3,2},{0,3},{5,4},{6,5},{7,6},{4,7},{9,8},{10,9},{11,1... | collective-permute-start | bytes 294920 | tf_op jit(solution)/shard_map/ppermute | solution.py:897
  15.3 1.4 %all-to-all-done.asked = f32[8,24,128]{2,1,0:T(8,128)S(1)} async-done(((f32[8,24,128]{2,1,0:T(8,128)}), f32[8,24,128]{2,1,0:T(8,128)S(1)}, u32[]{:S(2)}, u32[]{:S(2)}) %all-to-all-start) | async-done | bytes 98336 | tf_op jit(solution)/shard_map/all_to_all | solution.py:890
  16.7 0.2 corner.1
  16.9 0.1 collective-permute-start.2
  16.9 1.7 %collective-permute-start.3 = (f32[24,128]{1,0:T(8,128)S(1)}, f32[24,128]{1,0:T(8,128)S(1)}, u32[]{:S(2)}, u32[]{:S(2)}) collective-permute-start(f32[24,128]{1,0:T(8,128)S(1)} %get-tuple-element.25), channel_id=1, source_target_pairs={{1,0},{2,1},{3,2},{0,3},{5,4},{6,5},{7,6},{4,7},{9,8},{10,9},{11,1... | collective-permute-start | bytes 36872 | tf_op jit(solution)/shard_map/ppermute | solution.py:897
  18.7 0.0 collective-permute-done.low_main
  18.7 0.0 collective-permute-done.1.high_main
  18.7 1.4 %collective-permute-done.2.low_ext = f32[24,128]{1,0:T(8,128)S(1)} collective-permute-done((f32[24,128]{1,0:T(8,128)S(1)}, f32[24,128]{1,0:T(8,128)S(1)}, u32[]{:S(2)}, u32[]{:S(2)}) %collective-permute-start.2) | collective-permute-done | bytes 12320 | tf_op jit(solution)/shard_map/ppermute | solution.py:896
  20.1 0.0 collective-permute-done.3.high_ext
  20.1 4.5 %ghost.1 = (f32[16,8,128]{2,1,0:T(8,128)}, f32[1024,128]{1,0:T(8,128)}, s32[16]{0:T(128)S(4)}) custom-call(f32[9,32,32,128]{3,2,1,0:T(8,128)} %bitcast.3, f32[8,24,128]{2,1,0:T(8,128)S(1)} %all-to-all-done.asked, f32[3,9,8,1024]{3,2,1,0:T(8,128)S(1)} %get-tuple-element.20.sets_main, f32[24,1024]{1,0:T(8,128)S(1)} %collective-permute-done.low_main, ...), custom_call_target="tpu_custom_call" | custom-call | tf_op jit(solution)/shard_map/ghost/pallas_call | solution.py:936
  24.6 4.7 %all-to-all-start.1 = ((f32[16,8,128]{2,1,0:T(8,128)}), f32[16,8,128]{2,1,0:T(8,128)S(1)}, u32[]{:S(2)}, u32[]{:S(2)}) async-start(f32[16,8,128]{2,1,0:T(8,128)} %get-tuple-element.29), calls=%async_computation.1 | async-start | bytes 131072 | tf_op jit(solution)/shard_map/all_to_all | solution.py:968
  29.3 2.9 %start.1.post = f32[9,16,4096]{2,1,0:T(8,128)S(1)} custom-call(s32[64]{0:T(128)S(4)} %get-tuple-element.28.slot, f32[9,16,4096]{2,1,0:T(8,128)} %bitcast.4), custom_call_target="tpu_custom_call" | custom-call | tf_op jit(solution)/shard_map/start/pallas_call | solution.py:927
  32.2 4.2 %all-to-all-done.1.ghosts = f32[16,8,128]{2,1,0:T(8,128)S(1)} async-done(((f32[16,8,128]{2,1,0:T(8,128)}), f32[16,8,128]{2,1,0:T(8,128)S(1)}, u32[]{:S(2)}, u32[]{:S(2)}) %all-to-all-start.1) | async-done | bytes 65568 | tf_op jit(solution)/shard_map/all_to_all | solution.py:968
  36.4 4.9 %fine.1 = (f32[9,16,4096]{2,1,0:T(8,128)}, f32[16,72,128]{2,1,0:T(8,128)}) custom-call(s32[64]{0:T(128)S(4)} %get-tuple-element.28.slot, f32[9,16,4096]{2,1,0:T(8,128)S(1)} %start.1.post, f32[16,8,128]{2,1,0:T(8,128)S(1)} %all-to-all-done.1.ghosts), custom_call_target="tpu_custom_call" | custom-call | tf_op jit(solution)/shard_map/fine/pallas_call | solution.py:969
  41.3 3.5 %all-to-all-start.2 = ((f32[16,72,128]{2,1,0:T(8,128)}), f32[16,72,128]{2,1,0:T(8,128)S(1)}, u32[]{:S(2)}, u32[]{:S(2)}) async-start(f32[16,72,128]{2,1,0:T(8,128)} %get-tuple-element.30.after), calls=%async_computation.2 | async-start | bytes 1179648 | tf_op jit(solution)/shard_map/all_to_all | solution.py:987
  44.9 9.3 %coarse.6 = (f32[9,1024,128]{2,1,0:T(8,128)}, f32[9,512,128]{2,1,0:T(8,128)S(1)}, s32[32]{0:T(128)S(4)}) custom-call(f32[9,1024,128]{2,1,0:T(8,128)} %coarse.7, f32[8,24,128]{2,1,0:T(8,128)S(1)} %all-to-all-done.asked, f32[1024,128]{1,0:T(8,128)} %get-tuple-element.27.inject_hbm, f32[16,72,128]{2,1,0:T(8,128)} %get-tuple-element.30.after, ...), custom_call_target="tpu_custom_call" | custom-call | tf_op jit(solution)/shard_map/coarse/pallas_call | solution.py:988
  54.2 7.1 %all-to-all-done.2.back = f32[16,72,128]{2,1,0:T(8,128)S(1)} async-done(((f32[16,72,128]{2,1,0:T(8,128)}), f32[16,72,128]{2,1,0:T(8,128)S(1)}, u32[]{:S(2)}, u32[]{:S(2)}) %all-to-all-start.2) | async-done | bytes 589856 | tf_op jit(solution)/shard_map/all_to_all | solution.py:987
  61.3 2.5 %patch.1 = (f32[9,512,128]{2,1,0:T(8,128)S(1)}, f32[9,1024,128]{2,1,0:T(8,128)}) custom-call(s32[16]{0:T(128)S(4)} %get-tuple-element.26.ids, s32[32]{0:T(128)S(4)} %get-tuple-element.31.home, f32[9,1024,128]{2,1,0:T(8,128)} %get-tuple-element.32.base, f32[9,512,128]{2,1,0:T(8,128)S(1)} %get-tuple-element.33.strips_in, ...), custom_call_target="tpu_custom_call", output_to_operand_aliasing={{1}: (2, {}), {0}: (3, {})} | custom-call | tf_op jit(solution)/shard_map/patch/pallas_call | solution.py:1008
Async XLA Ops:
  2.3 14.4 %all-to-all-start = ((f32[8,24,128]{2,1,0:T(8,128)}), f32[8,24,128]{2,1,0:T(8,128)S(1)}, u32[]{:S(2)}, u32[]{:S(2)}) async-start(f32[8,24,128]{2,1,0:T(8,128)} %get-tuple-element.19), calls=%async_computation | async-start | bytes 196608 | tf_op jit(solution)/shard_map/all_to_all | solution.py:890
  13.5 5.2 %collective-permute-start = (f32[24,1024]{1,0:T(8,128)S(1)}, f32[24,1024]{1,0:T(8,128)S(1)}, u32[]{:S(2)}, u32[]{:S(2)}) collective-permute-start(f32[24,1024]{1,0:T(8,128)S(1)} %get-tuple-element.21), channel_id=1, source_target_pairs={{0,1},{1,2},{2,3},{3,0},{4,5},{5,6},{6,7},{7,4},{8,9},{9,10},{10,1... | collective-permute-start | bytes 294920 | tf_op jit(solution)/shard_map/ppermute | solution.py:896
  13.6 5.1 %collective-permute-start.1 = (f32[24,1024]{1,0:T(8,128)S(1)}, f32[24,1024]{1,0:T(8,128)S(1)}, u32[]{:S(2)}, u32[]{:S(2)}) collective-permute-start(f32[24,1024]{1,0:T(8,128)S(1)} %get-tuple-element.22), channel_id=1, source_target_pairs={{1,0},{2,1},{3,2},{0,3},{5,4},{6,5},{7,6},{4,7},{9,8},{10,9},{11,1... | collective-permute-start | bytes 294920 | tf_op jit(solution)/shard_map/ppermute | solution.py:897
  16.9 3.2 %collective-permute-start.2 = (f32[24,128]{1,0:T(8,128)S(1)}, f32[24,128]{1,0:T(8,128)S(1)}, u32[]{:S(2)}, u32[]{:S(2)}) collective-permute-start(f32[24,128]{1,0:T(8,128)S(1)} %get-tuple-element.24), channel_id=1, source_target_pairs={{0,1},{1,2},{2,3},{3,0},{4,5},{5,6},{6,7},{7,4},{8,9},{9,10},{10,1... | collective-permute-start | bytes 36872 | tf_op jit(solution)/shard_map/ppermute | solution.py:896
  16.9 3.1 %collective-permute-start.3 = (f32[24,128]{1,0:T(8,128)S(1)}, f32[24,128]{1,0:T(8,128)S(1)}, u32[]{:S(2)}, u32[]{:S(2)}) collective-permute-start(f32[24,128]{1,0:T(8,128)S(1)} %get-tuple-element.25), channel_id=1, source_target_pairs={{1,0},{2,1},{3,2},{0,3},{5,4},{6,5},{7,6},{4,7},{9,8},{10,9},{11,1... | collective-permute-start | bytes 36872 | tf_op jit(solution)/shard_map/ppermute | solution.py:897
  24.6 11.8 %all-to-all-start.1 = ((f32[16,8,128]{2,1,0:T(8,128)}), f32[16,8,128]{2,1,0:T(8,128)S(1)}, u32[]{:S(2)}, u32[]{:S(2)}) async-start(f32[16,8,128]{2,1,0:T(8,128)} %get-tuple-element.29), calls=%async_computation.1 | async-start | bytes 131072 | tf_op jit(solution)/shard_map/all_to_all | solution.py:968
  41.3 20.0 %all-to-all-start.2 = ((f32[16,72,128]{2,1,0:T(8,128)}), f32[16,72,128]{2,1,0:T(8,128)S(1)}, u32[]{:S(2)}, u32[]{:S(2)}) async-start(f32[16,72,128]{2,1,0:T(8,128)} %get-tuple-element.30.after), calls=%async_computation.2 | async-start | bytes 1179648 | tf_op jit(solution)/shard_map/all_to_all | solution.py:987
